TPU v7x, 512 devices: a whole 4x8x8 slice. The times are simulated.
512 devices in a mesh: seq: 64 (over z, y), tp: 8 (over x, core).
Axes of the slice: x: 4, y: 8, z: 8, core: 2. Of those that a mesh axis runs over, the one named last changes fastest.
Arguments:
- tokens: bfloat16 [384, 2048], P('seq', 'tp'), may hold values from -6 to 6
- norm_gain: float32 [2048], replicated, may hold values from 0.25 to 4
- w_query: bfloat16 [2048, 2048], P(None, 'tp'), may hold values from -0.125 to 0.125
- w_key_value: bfloat16 [2, 2048, 1024], P(None, None, 'tp'), may hold values from -0.125 to 0.125
- w_out: bfloat16 [2048, 2048], P('tp'), may hold values from -0.125 to 0.125
- kv_pool: bfloat16 [2, 7168, 16, 1024], P(None, 'seq', None, 'tp'), may hold values from -256 to 256
- slot_owner: int32 [7168, 2], P('seq'), may hold values from -1 to 1791, as said below
- slot_dest: int32 [7168], P('seq'), may hold values from -1 to 7167, as said below
- lengths: int32 [96], replicated, may hold values from 1 to 28668, as said below
Outputs:
- attn_out: bfloat16 [384, 2048], P('seq', 'tp')
- kv_moved: bfloat16 [2, 7168, 16, 1024], P(None, 'seq', None, 'tp')
Inputs may be any that keep to these rules, and one draw needn't show every extreme that they name: `lengths`: two requests are long, at least 22934 and one of them exactly 28668; the others hold at most 444. `slot_owner`: pages 0 to (lengths[r] + 3) // 16 of every request r are held by exactly one slot each, no other pages by any; a free slot holds (-1, -1). `slot_dest`: -1 where the page stays. Destinations are distinct, each a free slot or a slot whose own page moves. At most 2 slots of one index of seq move to slots of one index of seq, and exactly 2 do for some pair in every draw.
All inputs are finite; a program needn't handle non-finite values.
Results may differ from a plain program's by a relative error of at most 0.024.
The roundings to bfloat16 on the way count: a program that leaves them out, or rounds other values in their place, can miss the bound.
Values may be sent and summed in bfloat16 or wider, within the bound.
A program may use at most 128 MiB of HBM per device.

v0:
```python
import jax
import jax.numpy as jnp
from jax import lax
from jax.sharding import PartitionSpec as P

HD = 128
STEPS = 4


ROPE_BASE = 1000000.0
NEG_FILL = -1e30
NORM_EPS = 1e-06


def rotate(projected, positions, head_count):
    row_count = projected.shape[0]
    width = projected.shape[1] // head_count
    half_width = width // 2
    heads_view = projected.reshape(row_count, head_count, width)
    frequency = ROPE_BASE ** (-jnp.arange(half_width, dtype=jnp.float32) * 2.0 / width)
    angles = positions.astype(jnp.float32)[:, None] * frequency[None, :]
    cosine = jnp.cos(angles)[:, None, :]
    sine_part = jnp.sin(angles)[:, None, :]
    lower_half = heads_view[:, :, :half_width]
    upper_half = heads_view[:, :, half_width:]
    turned = jnp.concatenate(
        [
            lower_half * cosine - upper_half * sine_part,
            upper_half * cosine + lower_half * sine_part,
        ],
        axis=2,
    )
    return turned.reshape(row_count, head_count * width)


def project_rows(token_block, norm_gain, w_query, w_key_value, lengths):
    row_count = token_block.shape[0]
    row_index = jnp.arange(row_count, dtype=jnp.int32)
    positions = lengths[row_index // STEPS] + row_index % STEPS
    widened = token_block.astype(jnp.float32)
    mean_square = jnp.mean(widened * widened, axis=1, keepdims=True)
    normed = (widened * lax.rsqrt(mean_square + NORM_EPS) * norm_gain[None, :]).astype(jnp.bfloat16)
    queries = jnp.dot(normed, w_query, preferred_element_type=jnp.float32)
    keyval = jnp.einsum("rd,cde->cre", normed, w_key_value, preferred_element_type=jnp.float32)
    queries = rotate(queries, positions, w_query.shape[1] // HD).astype(jnp.bfloat16)
    fresh_key = rotate(keyval[0], positions, w_key_value.shape[2] // HD).astype(jnp.bfloat16)
    fresh_value = keyval[1].astype(jnp.bfloat16)
    return jnp.concatenate([queries, fresh_key, fresh_value], axis=1)


def local(tokens, norm_gain, w_query, w_key_value, w_out, kv_pool, slot_owner, slot_dest, lengths):
    seq_count = lax.axis_size("seq")
    my_index = lax.axis_index("seq")
    row_count = tokens.shape[0]
    slot_count = kv_pool.shape[1]
    page_size = kv_pool.shape[2]
    kv_width = kv_pool.shape[3]
    kv_count = kv_width // HD
    q_width = w_query.shape[1]
    q_count = q_width // HD
    group_size = q_count // kv_count
    request_count = lengths.shape[0]
    own_tokens = lax.all_gather(tokens, "tp", axis=1, tiled=True)
    packed = project_rows(
        lax.all_gather(own_tokens, "seq", axis=0, tiled=True),
        norm_gain,
        w_query,
        w_key_value,
        lengths,
    )
    query_all = packed[:, :q_width]
    key_new = packed[:, q_width : q_width + kv_width]
    value_new = packed[:, q_width + kv_width :]
    owner_req = slot_owner[:, 0]
    owner_page = slot_owner[:, 1]
    occupied = owner_req >= 0
    safe_req = jnp.where(occupied, owner_req, 0)
    base_len = lengths[safe_req]
    offset = jnp.arange(page_size, dtype=jnp.int32)
    position = owner_page[:, None] * page_size + offset[None, :]
    step_of = position - base_len[:, None]
    is_new = occupied[:, None] & (step_of >= 0) & (step_of < STEPS)
    source_row = jnp.where(is_new, safe_req[:, None] * STEPS + step_of, 0)
    fresh_rows = jnp.stack([key_new[source_row], value_new[source_row]])
    written = jnp.where(is_new[None, :, :, None], fresh_rows, kv_pool)
    slot_queries = query_all.reshape(request_count, STEPS, q_width)[safe_req]
    slot_queries = slot_queries.reshape(slot_count, STEPS, kv_count, group_size, HD)
    page_keys = written[0].reshape(slot_count, page_size, kv_count, HD)
    page_values = written[1].reshape(slot_count, page_size, kv_count, HD)
    scores = jnp.einsum(
        "stkgd,spkd->stkgp", slot_queries, page_keys, preferred_element_type=jnp.float32
    ) * HD ** (-0.5)
    step_ids = jnp.arange(STEPS, dtype=jnp.int32)
    visible = occupied[:, None, None] & (
        position[:, None, :] <= base_len[:, None, None] + step_ids[None, :, None]
    )
    visible = visible[:, :, None, None, :]
    scores = jnp.where(visible, scores, NEG_FILL)
    slot_top = jnp.max(scores, axis=4).reshape(slot_count, -1)
    member = owner_req[None, :] == jnp.arange(request_count, dtype=jnp.int32)[:, None]
    req_top = jnp.max(jnp.where(member[:, :, None], slot_top[None, :, :], NEG_FILL), axis=1)
    slot_ref = req_top[safe_req].reshape(slot_count, STEPS, kv_count, group_size, 1)
    weights = jnp.where(visible, jnp.exp(scores - slot_ref), 0.0)
    slot_sum = jnp.sum(weights, axis=4).reshape(slot_count, -1)
    slot_out = jnp.einsum(
        "stkgp,spkd->stkgd",
        weights.astype(jnp.bfloat16),
        page_values,
        preferred_element_type=jnp.float32,
    ).reshape(slot_count, -1)
    member_float = member.astype(jnp.float32)
    req_sum = jnp.dot(member_float, slot_sum, precision=lax.Precision.HIGHEST)
    req_out = jnp.dot(member_float, slot_out, precision=lax.Precision.HIGHEST)
    row_top = req_top.reshape(request_count * STEPS, q_count)
    row_sum = req_sum.reshape(request_count * STEPS, q_count)
    row_out = req_out.reshape(request_count * STEPS, q_width)
    first_own = my_index * row_count
    row_peak = lax.pmax(row_top, "seq")
    rescale = jnp.exp(row_top - row_peak)
    total_all, summed_all = lax.psum(
        (row_sum * rescale, row_out * jnp.repeat(rescale, HD, axis=1)), "seq"
    )
    row_total = lax.dynamic_slice_in_dim(total_all, first_own, row_count, 0)
    row_summed = lax.dynamic_slice_in_dim(summed_all, first_own, row_count, 0)
    attended = (row_summed / jnp.repeat(row_total, HD, axis=1)).astype(jnp.bfloat16)
    partial_out = jnp.dot(attended, w_out, preferred_element_type=jnp.float32)
    attn_out = lax.psum_scatter(
        partial_out.astype(jnp.bfloat16), "tp", scatter_dimension=1, tiled=True
    )
    moving = slot_dest >= 0
    capacity = -(-slot_count // seq_count)
    target_dev = jnp.where(moving, slot_dest // slot_count, -1)
    dev_hot = (target_dev[:, None] == jnp.arange(seq_count, dtype=jnp.int32)[None, :]).astype(
        jnp.int32
    )
    send_rank = jnp.sum((jnp.cumsum(dev_hot, axis=0) - 1) * dev_hot, axis=1)
    buffer_slot = jnp.where(moving, target_dev * capacity + send_rank, -1)
    picker = (
        buffer_slot[None, :] == jnp.arange(seq_count * capacity, dtype=jnp.int32)[:, None]
    ).astype(jnp.bfloat16)
    outgoing = jnp.einsum(
        "bs,cspw->cbpw", picker, written, preferred_element_type=jnp.float32
    ).astype(jnp.bfloat16)
    arrived = lax.all_to_all(outgoing, "seq", split_axis=1, concat_axis=1, tiled=True)
    every_dest = lax.all_gather(slot_dest, "seq", axis=0, tiled=True).reshape(seq_count, slot_count)
    to_me = (every_dest >= 0) & (every_dest // slot_count == my_index)
    arrival_rank = jnp.cumsum(to_me.astype(jnp.int32), axis=1) - 1
    local_slot = every_dest % slot_count
    matches = to_me[:, None, :] & (
        arrival_rank[:, None, :] == jnp.arange(capacity, dtype=jnp.int32)[None, :, None]
    )
    landing = jnp.sum(jnp.where(matches, local_slot[:, None, :], 0), axis=2).reshape(-1)
    filled = jnp.any(matches, axis=2).reshape(-1)
    placer = filled[None, :] & (
        landing[None, :] == jnp.arange(slot_count, dtype=jnp.int32)[:, None]
    )
    incoming = jnp.einsum(
        "lb,cbpw->clpw", placer.astype(jnp.bfloat16), arrived, preferred_element_type=jnp.float32
    ).astype(jnp.bfloat16)
    landed = jnp.any(placer, axis=1)
    kv_moved = jnp.where(
        landed[None, :, None, None],
        incoming,
        jnp.where(moving[None, :, None, None], jnp.zeros_like(written), written),
    )
    return (attn_out, kv_moved)


def solution(mesh):
    in_specs = (
        P("seq", "tp"),
        P(),
        P(None, "tp"),
        P(None, None, "tp"),
        P("tp", None),
        P(None, "seq", None, "tp"),
        P("seq", None),
        P("seq"),
        P(),
    )
    out_specs = (P("seq", "tp"), P(None, "seq", None, "tp"))
    return jax.shard_map(local, mesh=mesh, in_specs=in_specs, out_specs=out_specs, check_vma=False)
```

profile of v0, /device:TPU:1, one launch (start us, length us, event | category | flops | bytes accessed | tf_op | source)
XLA Modules:
  0.0 962.3 jit_solution(14826974249514475669)
XLA Ops:
  7.3 20.7 %all_gather.9 = bf16[6,2048]{1,0:T(8,128)(2,1)} all-gather(bf16[6,256]{1,0:T(8,128)(2,1)} %param.9), channel_id=1, replica_groups=mesh['seq'=64,'tp'=8] {'tp'}, dimensions={1}, use_global_device_ids=true | all-gather | bytes 27648 | tf_op jit(solution)/shard_map/all_gather | solution.py:63
  30.1 1.3 dynamic-slice
  32.9 226.3 %all-reduce = s32[7168]{0:T(1024)S(1)} all-reduce(s32[7168]{0:T(1024)S(1)} %dynamic-update-slice), channel_id=1, replica_groups=mesh['seq'=64,'tp'=8] {'seq'}, use_global_device_ids=true, to_apply=%add | all-reduce | flops 7168 | bytes 57344
  259.3 1.6 gather_fusion
  261.1 3.4 gather_fusion.1
  270.6 4.0 reshape.637
  274.6 2.3 multiply_reduce_fusion
  280.8 1.5 gather_fusion.4
  283.0 3.7 gather_fusion.3
  286.8 3.7 gather_fusion.2
  291.9 1.5 fusion.65
  295.3 1.7 fusion
  297.0 1.7 copy.84
  298.7 4.7 all-to-all-start
  303.6 2.2 fusion.8
  308.5 1.5 convolution_bitcast_fusion
  311.4 1.4 fusion.44
  313.7 226.9 %pmax.7 = f32[384,2]{1,0:T(8,128)S(1)} all-reduce(f32[384,2]{1,0:T(8,128)} %reshape.575), channel_id=1, replica_groups=mesh['seq'=64,'tp'=8] {'seq'}, use_global_device_ids=true, to_apply=%region_3.4 | all-reduce | flops 768 | bytes 6144 | tf_op jit(solution)/shard_map/pmax | solution.py:118
  542.1 1.8 bitcast_multiply_fusion
  544.1 219.7 %psum.15 = f32[384,2]{1,0:T(8,128)S(1)} all-reduce(f32[384,2]{1,0:T(8,128)S(1)} %get-tuple-element.4), channel_id=1, replica_groups=mesh['seq'=64,'tp'=8] {'seq'}, use_global_device_ids=true, to_apply=%region_6.7 | all-reduce | flops 768 | bytes 6144 | tf_op jit(solution)/shard_map/psum | solution.py:120
  763.9 32.8 %all-reduce.3.cloned.1.call-done = f32[384,256]{1,0:T(8,128)} async-done(((f32[384,256]{1,0:T(8,128)}), f32[384,256]{1,0:T(8,128)}) %all-reduce.3.cloned.1.call-update) | async-done | bytes 393232 | tf_op jit(solution)/shard_map/psum | solution.py:120
  796.7 2.1 convolution_convert_fusion
  799.3 3.8 fusion.6
  803.1 152.6 %reduce-scatter.2.cloned.1.call-done = bf16[6,256]{1,0:T(8,128)(2,1)} async-done(((bf16[6,2048]{1,0:T(8,128)(2,1)}), bf16[6,256]{1,0:T(8,128)(2,1)}) %reduce-scatter.2.cloned.1.call-update) | async-done | bytes 3088 | tf_op jit(solution)/shard_map/reduce_scatter | solution.py:127
  (112 shorter events, 24.5 us)
Async XLA Ops:
  7.2 271.2 %copy-start = (bf16[2048,256]{1,0:T(8,128)(2,1)S(1)}, bf16[2048,256]{1,0:T(8,128)(2,1)}, u32[]{:S(2)}) copy-start(bf16[2048,256]{1,0:T(8,128)(2,1)} %param.11) | copy-start | bytes 3145732
  7.2 261.6 %copy-start.10 = (s32[112,2]{0,1:T(2,128)S(1)}, s32[112,2]{0,1:T(2,128)}, u32[]{:S(2)}) copy-start(s32[112,2]{0,1:T(2,128)} %param.15) | copy-start | bytes 2692
  7.2 261.0 %copy-start.12 = (s32[112]{0:T(128)S(1)}, s32[112]{0:T(128)}, u32[]{:S(2)}) copy-start(s32[112]{0:T(128)} %param.16) | copy-start | bytes 1348
  7.2 257.4 %copy-start.4 = (bf16[2,2048,128]{2,1,0:T(8,128)(2,1)S(1)}, bf16[2,2048,128]{2,1,0:T(8,128)(2,1)}, u32[]{:S(2)}) copy-start(bf16[2,2048,128]{2,1,0:T(8,128)(2,1)} %param.12) | copy-start | bytes 3145732
  7.2 263.4 %all-gather.3.cloned.1.call-start = ((), (), s32[]{:S(2)}) async-start(), calls=%async_computation.4 | async-start | bytes 2129920 | tf_op jit(solution)/shard_map/all_gather | solution.py:65
  259.3 21.6 %copy-start.7 = (s32[1024]{0:T(1024)}, s32[1024]{0:T(1024)S(1)}, u32[]{:S(2)}) copy-start(s32[1024]{0:T(1024)S(1)} %pad_clamp_fusion.2) | copy-start | bytes 12292
  269.8 21.1 %copy-start.5 = (pred[112,4,16]{2,1,0:T(4,128)(4,1)}, pred[112,4,16]{2,1,0:T(4,128)(4,1)S(1)}, u32[]{:S(2)}) copy-start(pred[112,4,16]{2,1,0:T(4,128)(4,1)S(1)} %compare_and_fusion) | copy-start | bytes 21508
  270.6 6.4 copy-start.6
  274.6 2.8 copy-start.1
  283.0 7.5 copy-start.3
  291.0 0.9 copy-start.2
  298.7 500.1 %all-to-all-start = ((bf16[2,128,16,128]{3,2,0,1:T(8,128)(2,1)}), bf16[2,128,16,128]{3,2,0,1:T(8,128)(2,1)S(1)}, u32[]{:S(2)}, u32[]{:S(2)}) async-start(bf16[2,128,16,128]{3,2,0,1:T(8,128)(2,1)} %copy.84), calls=%async_computation.1 | async-start | bytes 2097152 | tf_op jit(solution)/shard_map/all_to_all | solution.py:144
  303.4 493.3 %all-reduce.3.cloned.1.call-start = ((), (), s32[]{:S(2)}) async-start(), calls=%async_computation.2 | async-start | bytes 786432 | tf_op jit(solution)/shard_map/psum | solution.py:120
  310.3 233.7 %copy-start.8 = (s32[128]{0:T(128)S(1)}, s32[128]{0:T(128)}, u32[]{:S(2)}) copy-start(s32[128]{0:T(128)} %eq.100) | copy-start | bytes 1540
  310.3 233.7 %copy-start.9 = (pred[128]{0:T(512)(128)(4,1)S(1)}, pred[128]{0:T(512)(128)(4,1)}, u32[]{:S(2)}) copy-start(pred[128]{0:T(512)(128)(4,1)} %and.153) | copy-start | bytes 388
  540.5 258.8 %copy-start.11 = (pred[112]{0:T(512)(128)(4,1)S(1)}, pred[112]{0:T(512)(128)(4,1)}, u32[]{:S(2)}) copy-start(pred[112]{0:T(512)(128)(4,1)} %broadcast_compare_fusion.2) | copy-start | bytes 340
  543.9 411.9 %reduce-scatter.2.cloned.1.call-start = ((), (), s32[]{:S(2)}) async-start(), calls=%async_computation.3 | async-start | bytes 36864 | tf_op jit(solution)/shard_map/reduce_scatter | solution.py:127
Sparse Core Ops, SparseCore 0:
  28.1 77.8 all-gather.2
  544.0 252.6 all-reduce.2
  800.0 155.6 reduce-scatter.1
where the time goes:
time: 963 us; the launch traced here: 962 us
  blocking collectives  694 us (72%)
  waiting for transfers between devices  186 us (19%)
  local copies, waits for them, and re-layouts  33.9 us (4%)
  other arithmetic  18.9 us (2%)
  between operations  14.9 us (2%)
  matrix products  10.5 us (1%)
    pmax x1, blocking collectives, local(): row_peak = lax.pmax(row_top, 'seq')  227 us
    unnamed x1, blocking collectives  226 us
    psum x1, blocking collectives, local(): lax.psum((row_sum * rescale, row_out * jnp.repeat(rescale, HD, axis=1)),...  220 us
    reduce_scatter x1, waiting for transfers between devices, local(): lax.psum_scatter(partial_out.astype(jnp.bfloat16), 'tp', scatter_dimensio...  153 us
    psum x1, waiting for transfers between devices, local(): lax.psum((row_sum * rescale, row_out * jnp.repeat(rescale, HD, axis=1)),...  32.8 us
    all_gather x1, blocking collectives, local(): own_tokens = lax.all_gather(tokens, 'tp', axis=1, tiled=True)  20.7 us
  transfers between devices with their start and end apart: 4, of which 2 were waited for; matrix products, arithmetic and copies ran while one was open for 4% of the time, Pallas kernels for 0%

commit v1 on v0

v1 whole, which is shorter than its diff:
```python
import functools

import jax
import jax.numpy as jnp
from jax import lax
from jax.experimental import pallas as pl
from jax.experimental.pallas import tpu as pltpu
from jax.sharding import PartitionSpec as P

HD = 128
STEPS = 4
PADDED = 8
ROPE_BASE = 1000000.0
NEG_FILL = -1e30
NORM_EPS = 1e-06
VMEM = pltpu.VMEM
SMEM = pltpu.SMEM


def in_vmem():
    return pl.BlockSpec(memory_space=VMEM)


def in_smem():
    return pl.BlockSpec(memory_space=SMEM)


def take(table, index):
    ids = jnp.arange(table.shape[0], dtype=jnp.int32)
    return jnp.sum(jnp.where(index[:, None] == ids[None, :], table[None, :], 0), axis=1)


def rotate(projected, positions, head_count):
    row_count = projected.shape[0]
    width = projected.shape[1] // head_count
    half_width = width // 2
    heads_view = projected.reshape(row_count, head_count, width)
    frequency = ROPE_BASE ** (-jnp.arange(half_width, dtype=jnp.float32) * 2.0 / width)
    angles = positions.astype(jnp.float32)[:, None] * frequency[None, :]
    cosine = jnp.cos(angles)[:, None, :]
    sine_part = jnp.sin(angles)[:, None, :]
    lower_half = heads_view[:, :, :half_width]
    upper_half = heads_view[:, :, half_width:]
    turned = jnp.concatenate(
        [
            lower_half * cosine - upper_half * sine_part,
            upper_half * cosine + lower_half * sine_part,
        ],
        axis=2,
    )
    return turned.reshape(row_count, head_count * width)


def project_rows(token_block, norm_gain, w_query, w_key_value, positions):
    widened = token_block.astype(jnp.float32)
    mean_square = jnp.mean(widened * widened, axis=1, keepdims=True)
    normed = (widened * lax.rsqrt(mean_square + NORM_EPS) * norm_gain[None, :]).astype(jnp.bfloat16)
    queries = jnp.dot(normed, w_query, preferred_element_type=jnp.float32)
    keys = jnp.dot(normed, w_key_value[0], preferred_element_type=jnp.float32)
    values = jnp.dot(normed, w_key_value[1], preferred_element_type=jnp.float32)
    queries = rotate(queries, positions, w_query.shape[1] // HD).astype(jnp.bfloat16)
    fresh_key = rotate(keys, positions, w_key_value.shape[2] // HD).astype(jnp.bfloat16)
    return jnp.concatenate([queries, fresh_key, values.astype(jnp.bfloat16)], axis=1)


def pick_kernel(source_ref, pool_ref, out_ref):
    @pl.loop(0, out_ref.shape[0])
    def _(b):
        s = source_ref[b]
        out_ref[b, 0] = pool_ref[0, s]
        out_ref[b, 1] = pool_ref[1, s]


def overlay(base, source, fresh_all):
    rows = base.shape[0]
    ids = lax.broadcasted_iota(jnp.int32, (rows, fresh_all.shape[0]), 1)
    hot = jnp.where(ids == source, 1.0, 0.0).astype(jnp.bfloat16)
    fresh = jnp.dot(hot, fresh_all, preferred_element_type=jnp.float32)
    return jnp.where(source >= 0, fresh, base.astype(jnp.float32)).astype(jnp.bfloat16)


def attend_kernel(
    packed_ref, pool_ref, source_ref, owner_ref, pos_ref, req_ref, limit_ref, meta_ref,
    out_ref, keys, values,
):
    slots, page = pool_ref.shape[1], pool_ref.shape[2]
    entries = slots * page
    chunk_slots = 16
    chunk = chunk_slots * page

    @pl.loop(0, slots // chunk_slots)
    def _(c):
        at = pl.ds(pl.multiple_of(c * chunk, chunk), chunk)
        source = source_ref[at, :]
        for half, into in ((0, keys), (1, values)):
            base = pool_ref[half, pl.ds(c * chunk_slots, chunk_slots)].reshape(chunk, HD)
            fresh_all = packed_ref[:, (2 + half) * HD : (3 + half) * HD]
            into[at, :] = overlay(base, source, fresh_all)

    block = 64

    @pl.loop(0, packed_ref.shape[0] // block)
    def _(b):
        at = pl.ds(pl.multiple_of(b * block, block), block)
        visible = (owner_ref[...] == req_ref[at, :]) & (pos_ref[...] <= limit_ref[at, :])
        lane = lax.broadcasted_iota(jnp.int32, (block, HD), 1)
        stats = meta_ref[at, :]
        for g in range(2):
            query = packed_ref[at, g * HD : (g + 1) * HD]
            scores = lax.dot_general(
                query, keys[...], (((1,), (1,)), ((), ())), preferred_element_type=jnp.float32
            ) * HD ** (-0.5)
            scores = jnp.where(visible, scores, NEG_FILL)
            top = jnp.max(scores, axis=1, keepdims=True)
            weights = jnp.where(visible, jnp.exp(scores - top), 0.0)
            total = jnp.sum(weights, axis=1, keepdims=True)
            out_ref[at, g * HD : (g + 1) * HD] = jnp.dot(
                weights.astype(jnp.bfloat16), values[...], preferred_element_type=jnp.float32
            )
            stats = jnp.where(lane == g, top, jnp.where(lane == 2 + g, total, stats))
        out_ref[at, 2 * HD : 3 * HD] = stats


def place_kernel(from_ref, arrived_ref, pool_ref, source_ref, packed_ref, out_ref, base):
    slots, page = pool_ref.shape[1], pool_ref.shape[2]

    @pl.loop(0, slots)
    def _(g):
        s = from_ref[g]

        @pl.when(s >= 0)
        def _():
            base[0, g] = arrived_ref[s, 0]
            base[1, g] = arrived_ref[s, 1]

        @pl.when(s == -1)
        def _():
            base[0, g] = pool_ref[0, g]
            base[1, g] = pool_ref[1, g]

        @pl.when(s < -1)
        def _():
            base[0, g] = jnp.zeros_like(base[0, g])
            base[1, g] = jnp.zeros_like(base[1, g])

    chunk_slots = 16
    chunk = chunk_slots * page

    @pl.loop(0, slots // chunk_slots)
    def _(c):
        source = source_ref[pl.ds(pl.multiple_of(c * chunk, chunk), chunk), :]
        for half in range(2):
            at = pl.ds(c * chunk_slots, chunk_slots)
            fresh_all = packed_ref[:, (2 + half) * HD : (3 + half) * HD]
            out_ref[half, at] = overlay(
                base[half, at].reshape(chunk, HD), source, fresh_all
            ).reshape(chunk_slots, page, HD)


def new_sources(req, page, lengths, page_size, own_rows):
    base_len = take(lengths, req)
    offset = jnp.arange(page_size, dtype=jnp.int32)
    position = page[:, None] * page_size + offset[None, :]
    step_of = position - base_len[:, None]
    is_new = (req >= 0)[:, None] & (step_of >= 0) & (step_of < STEPS)
    row = req[:, None] * STEPS + step_of
    padded_row = row // own_rows * PADDED + row % own_rows
    return position, jnp.where(is_new, padded_row, -1)


def local(tokens, norm_gain, w_query, w_key_value, w_out, kv_pool, slot_owner, slot_dest, lengths):
    seq_count = lax.axis_size("seq")
    my_index = lax.axis_index("seq")
    own_rows = tokens.shape[0]
    slot_count = kv_pool.shape[1]
    page_size = kv_pool.shape[2]
    entries = slot_count * page_size
    capacity = -(-slot_count // seq_count)
    i32 = jnp.int32

    moving = slot_dest >= 0
    target_dev = jnp.where(moving, slot_dest // slot_count, -1)
    slot_ids = jnp.arange(slot_count, dtype=i32)
    same = (target_dev[None, :] == target_dev[:, None]) & (slot_ids[None, :] < slot_ids[:, None])
    send_rank = jnp.sum(same.astype(i32), axis=1)
    buffer_slot = jnp.where(moving, target_dev * capacity + send_rank, -1)
    hot = buffer_slot[None, :] == jnp.arange(seq_count * capacity, dtype=i32)[:, None]
    filled = jnp.any(hot, axis=1)

    def picked(values):
        return jnp.sum(jnp.where(hot, values[None, :], 0), axis=1)

    pick_slot = picked(slot_ids)
    outgoing = pl.pallas_call(
        pick_kernel,
        out_shape=jax.ShapeDtypeStruct(
            (seq_count * capacity, 2, page_size, HD), jnp.bfloat16
        ),
        in_specs=[in_smem(), in_vmem()],
        out_specs=in_vmem(),
        name="pick_pages",
    )(pick_slot, kv_pool)
    arrived = lax.all_to_all(outgoing, "seq", split_axis=0, concat_axis=0, tiled=True)
    meta = jnp.stack(
        [
            jnp.where(filled, picked(slot_dest % slot_count), -1),
            picked(slot_owner[:, 0]),
            picked(slot_owner[:, 1]),
        ],
        axis=1,
    ).astype(jnp.float32)
    meta = meta.reshape(seq_count, 1, capacity * 3)
    meta = jnp.pad(meta, ((0, 0), (0, 0), (4, HD - 4 - capacity * 3)))
    meta = jnp.broadcast_to(meta, (seq_count, PADDED, HD)).reshape(seq_count * PADDED, HD)

    own_tokens = lax.all_gather(tokens, "tp", axis=1, tiled=True)
    own_tokens = jnp.pad(own_tokens, ((0, PADDED - own_rows), (0, 0)))
    own_index = my_index * own_rows + jnp.arange(PADDED, dtype=i32)
    own_positions = take(lengths, own_index // STEPS) + own_index % STEPS
    own_packed = project_rows(own_tokens, norm_gain, w_query, w_key_value, own_positions)
    packed = lax.all_gather(own_packed[None], "seq", axis=0, tiled=True)
    packed = packed.reshape(seq_count * PADDED, own_packed.shape[1])

    padded_ids = jnp.arange(seq_count * PADDED, dtype=i32)
    row_of = padded_ids // PADDED * own_rows + padded_ids % PADDED
    real = padded_ids % PADDED < own_rows
    row_req = jnp.where(real, row_of // STEPS, -2)
    row_limit = take(lengths, row_req) + row_of % STEPS
    position, source = new_sources(
        slot_owner[:, 0], slot_owner[:, 1], lengths, page_size, own_rows
    )
    entry_owner = jnp.broadcast_to(slot_owner[:, :1], (slot_count, page_size))

    partials = pl.pallas_call(
        attend_kernel,
        out_shape=jax.ShapeDtypeStruct((seq_count * PADDED, 3 * HD), jnp.float32),
        in_specs=[in_vmem()] * 8,
        out_specs=in_vmem(),
        scratch_shapes=[VMEM((entries, HD), jnp.bfloat16)] * 2,
        name="attend",
    )(
        packed,
        kv_pool,
        source.reshape(entries, 1),
        entry_owner.reshape(1, entries),
        position.reshape(1, entries),
        row_req[:, None],
        row_limit[:, None],
        meta,
    )
    gathered = lax.all_to_all(
        partials.reshape(seq_count, PADDED, 3 * HD), "seq", split_axis=0, concat_axis=0, tiled=True
    )
    stats = gathered[:, :, 2 * HD :]
    top = stats[:, :, 0:2]
    peak = jnp.max(top, axis=0, keepdims=True)
    rescale = jnp.exp(top - peak)
    total = jnp.sum(stats[:, :, 2:4] * rescale, axis=0)
    summed = jnp.sum(gathered[:, :, : 2 * HD] * jnp.repeat(rescale, HD, axis=2), axis=0)
    total = jnp.where(total > 0.0, total, 1.0)
    attended = (summed / jnp.repeat(total, HD, axis=1)).astype(jnp.bfloat16)
    partial_out = jnp.dot(attended, w_out, preferred_element_type=jnp.float32)
    attn_out = lax.psum_scatter(
        partial_out[:own_rows].astype(jnp.bfloat16), "tp", scatter_dimension=1, tiled=True
    )

    came = stats[:, 0, 4 : 4 + capacity * 3].astype(i32).reshape(seq_count * capacity, 3)
    lands = came[None, :, 0] == slot_ids[:, None]
    landed = jnp.any(lands, axis=1)

    def landing(values):
        return jnp.sum(jnp.where(lands, values[None, :], 0), axis=1)

    stay_or_zero = jnp.where(moving, -2, -1)
    from_index = jnp.where(
        landed, landing(jnp.arange(seq_count * capacity, dtype=i32)), stay_or_zero
    )
    final_req = jnp.where(landed, landing(came[:, 1]), jnp.where(moving, -1, slot_owner[:, 0]))
    final_page = jnp.where(landed, landing(came[:, 2]), slot_owner[:, 1])
    _, final_source = new_sources(final_req, final_page, lengths, page_size, own_rows)
    kv_moved = pl.pallas_call(
        place_kernel,
        out_shape=jax.ShapeDtypeStruct(kv_pool.shape, kv_pool.dtype),
        in_specs=[in_smem()] + [in_vmem()] * 4,
        out_specs=in_vmem(),
        scratch_shapes=[VMEM(kv_pool.shape, kv_pool.dtype)],
        name="place_pages",
    )(from_index, arrived, kv_pool, final_source.reshape(entries, 1), packed)
    return (attn_out, kv_moved)


def solution(mesh):
    in_specs = (
        P("seq", "tp"),
        P(),
        P(None, "tp"),
        P(None, None, "tp"),
        P("tp", None),
        P(None, "seq", None, "tp"),
        P("seq", None),
        P("seq"),
        P(),
    )
    out_specs = (P("seq", "tp"), P(None, "seq", None, "tp"))
    return jax.shard_map(local, mesh=mesh, in_specs=in_specs, out_specs=out_specs, check_vma=False)
```

time: 963 us -> 194 us (0.20)
  blocking collectives: 694 us -> 63.8 us
  waiting for transfers between devices: 186 us -> 48.6 us
  Pallas kernels: 0 us -> 24.6 us
  local copies, waits for them, and re-layouts: 33.9 us -> 13.6 us
    pmax x1 -> x0, blocking collectives: 227 us -> none  [local(): row_peak = lax.pmax(row_top, 'seq')]
    unnamed x1 -> x0, blocking collectives: 226 us -> none
    psum x1 -> x0, blocking collectives: 220 us -> none  [local(): lax.psum((row_sum * rescale, row_out * jnp.repeat(rescale, HD, axis=1)),...]
    reduce_scatter x1, waiting for transfers between devices: 153 us -> 27.9 us  [local(): lax.psum_scatter(partial_out[:own_rows].astype(jnp.bfloat16), 'tp', scatt...]
    all_gather x0 -> x1, blocking collectives: none -> 44.1 us  [local(): packed = lax.all_gather(own_packed[None], 'seq', axis=0, tiled=True)]
    psum x1 -> x0, waiting for transfers between devices: 32.8 us -> none  [local(): lax.psum((row_sum * rescale, row_out * jnp.repeat(rescale, HD, axis=1)),...]
    pallas_call x0 -> x3, Pallas kernels: none -> 24.6 us  [the longest x1 13.8 us: local(): pl.pallas_call(attend_kernel, out_shape=jax.ShapeDtypeStruct((seq_count *...]
    all_to_all x1 -> x2, waiting for transfers between devices: 0.01 us -> 20.7 us  [the longest x1 13.6 us: local(): lax.all_to_all(partials.reshape(seq_count, PADDED, 3 * HD), 'seq', split_...]
  transfers between devices with their start and end apart: 4 -> 3, of which waited for: 2 -> 3; matrix products, arithmetic and copies ran while one was open for 4% -> 6% of each run, Pallas kernels for 0% -> 6%
where the time goes in v1:
time: 194 us; the launch traced here: 193 us
  blocking collectives  63.8 us (33%)
  waiting for transfers between devices  48.6 us (25%)
  Pallas kernels  24.6 us (13%)
  between operations  14.3 us (7%)
  local copies, waits for them, and re-layouts  13.6 us (7%)
  starting transfers between devices  13 us (7%)
  other arithmetic  10.9 us (6%)
  matrix products  3.76 us (2%)
    all_gather x1, blocking collectives, local(): packed = lax.all_gather(own_packed[None], 'seq', axis=0, tiled=True)  44.1 us
    reduce_scatter x1, waiting for transfers between devices, local(): lax.psum_scatter(partial_out[:own_rows].astype(jnp.bfloat16), 'tp', scatt...  27.9 us
    all_gather x1, blocking collectives, local(): own_tokens = lax.all_gather(tokens, 'tp', axis=1, tiled=True)  19.7 us
    pallas_call x1, Pallas kernels, local(): pl.pallas_call(attend_kernel, out_shape=jax.ShapeDtypeStruct((seq_count *...  13.8 us
    all_to_all x1, waiting for transfers between devices, local(): lax.all_to_all(partials.reshape(seq_count, PADDED, 3 * HD), 'seq', split_...  13.6 us
    pallas_call x1, Pallas kernels, local(): pl.pallas_call(place_kernel, out_shape=jax.ShapeDtypeStruct(kv_pool.shape...  7.89 us
    all_to_all x1, starting transfers between devices, local(): lax.all_to_all(partials.reshape(seq_count, PADDED, 3 * HD), 'seq', split_...  7.5 us
    all_to_all x1, waiting for transfers between devices, local(): lax.all_to_all(outgoing, 'seq', split_axis=0, concat_axis=0, tiled=True)  7.11 us
  transfers between devices with their start and end apart: 3, of which 3 were waited for; matrix products, arithmetic and copies ran while one was open for 6% of the time, Pallas kernels for 6%

profile of v1, /device:TPU:1, one launch (start us, length us, event | category | flops | bytes accessed | tf_op | source)
XLA Modules:
  0.0 192.6 jit_solution(2370406997588317929)
XLA Ops:
  7.2 0.8 compare_bitcast_fusion
  8.1 0.8 slice_bitcast_fusion
  8.8 19.7 %all_gather.6 = bf16[6,2048]{1,0:T(8,128)(2,1)S(1)} all-gather(bf16[6,256]{1,0:T(8,128)(2,1)} %param.9), channel_id=1, replica_groups=mesh['seq'=64,'tp'=8] {'tp'}, dimensions={1}, use_global_device_ids=true | all-gather | bytes 27648 | tf_op jit(solution)/shard_map/all_gather | solution.py:216
  28.6 1.3 convolution_convert_fusion
  29.9 1.3 convolution_bitcast_fusion.1
  34.7 0.7 reshape.634.owner_ref
  37.6 0.7 broadcast_bitcast_fusion.meta_ref
  39.0 1.1 fusion.19
  40.4 44.1 %all-gather.packed_ref = bf16[512,512]{1,0:T(8,128)(2,1)} all-gather(bf16[8,512]{1,0:T(8,128)(2,1)S(1)} %pad_maximum_fusion), channel_id=2, replica_groups=mesh['seq'=64,'tp'=8] {'seq'}, dimensions={0}, use_global_device_ids=true | all-gather | bytes 532480 | tf_op jit(solution)/shard_map/all_gather | solution.py:221
  85.4 1.5 fusion.2.source_ref
  86.9 13.8 %attend.1 = f32[512,384]{1,0:T(8,128)} custom-call(bf16[512,512]{1,0:T(8,128)(2,1)} %all-gather.packed_ref, bf16[2,112,16,128]{3,2,1,0:T(8,128)(2,1)} %pool_ref.5, s32[1792,1]{1,0:T(8,128)} %fusion.2.source_ref, s32[1,1792]{1,0:T(1,128)} %reshape.634.owner_ref, s32[1,1792]{1,0:T(1,128)} %add.317.pos_ref, s32[512,1]{1,0:T(8,128)} %get-tuple-element.41.req_ref, ...), custom_call_target="tpu_custom_call" | custom-call | tf_op jit(solution)/shard_map/attend/pallas_call | solution.py:234
  100.7 7.5 %all-to-all-start = ((f32[64,8,384]{2,1,0:T(8,128)}), f32[64,8,384]{2,1,0:T(8,128)S(1)}, u32[]{:S(2)}, u32[]{:S(2)}) async-start(f32[64,8,384]{2,1,0:T(8,128)} %bitcast.57), calls=%async_computation | async-start | bytes 1572864 | tf_op jit(solution)/shard_map/all_to_all | solution.py:251
  108.2 3.0 %pick_pages.1 = bf16[128,2,16,128]{3,2,1,0:T(8,128)(2,1)} custom-call(s32[128]{0:T(128)} %get-tuple-element.8.source_ref, bf16[2,112,16,128]{3,2,1,0:T(8,128)(2,1)} %pool_ref.5), custom_call_target="tpu_custom_call" | custom-call | tf_op jit(solution)/shard_map/pick_pages/pallas_call | solution.py:194
  111.2 13.6 %all-to-all-done = f32[64,8,384]{2,1,0:T(8,128)S(1)} async-done(((f32[64,8,384]{2,1,0:T(8,128)}), f32[64,8,384]{2,1,0:T(8,128)S(1)}, u32[]{:S(2)}, u32[]{:S(2)}) %all-to-all-start) | async-done | bytes 786464 | tf_op jit(solution)/shard_map/all_to_all | solution.py:251
  124.8 5.5 %all-to-all-start.1 = ((bf16[128,2,16,128]{3,2,1,0:T(8,128)(2,1)}), bf16[128,2,16,128]{3,2,1,0:T(8,128)(2,1)S(1)}, u32[]{:S(2)}, u32[]{:S(2)}) async-start(bf16[128,2,16,128]{3,2,1,0:T(8,128)(2,1)} %pick_pages.1), calls=%async_computation.2 | async-start | bytes 2097152 | tf_op jit(solution)/shard_map/all_to_all | solution.py:203
  132.5 1.3 reshape.650
  133.8 1.3 reshape.649
  136.2 0.9 fusion.49
  137.8 1.4 div.120
  139.2 2.7 %fusion.5.source_ref = s32[1792,1]{1,0:T(8,128)} fusion(pred[1792,1]{1,0:T(8,128)(4,1)S(1)} %copy-done.4, s32[1792,1]{1,0:T(8,128)} %div.120, s32[1792,1]{1,0:T(8,128)S(1)} %rem.184, pred[1792,1]{1,0:T(8,128)(4,1)S(1)} %copy-done.3), kind=kLoop, calls=%fused_computation.12 | loop fusion | flops 19712 | bytes 25088 | tf_op jit(solution)/shard_map/jit(_where)/select_n | solution.py:168
  141.9 7.1 %all-to-all-done.1.arrived_ref = bf16[128,2,16,128]{3,2,1,0:T(8,128)(2,1)S(1)} async-done(((bf16[128,2,16,128]{3,2,1,0:T(8,128)(2,1)}), bf16[128,2,16,128]{3,2,1,0:T(8,128)(2,1)S(1)}, u32[]{:S(2)}, u32[]{:S(2)}) %all-to-all-start.1) | async-done | bytes 1048608 | tf_op jit(solution)/shard_map/all_to_all | solution.py:203
  149.0 1.0 copy-done.1
  150.0 7.9 %place_pages.1 = bf16[2,112,16,128]{3,2,1,0:T(8,128)(2,1)} custom-call(s32[112]{0:T(128)} %get-tuple-element.29.from_ref, bf16[128,2,16,128]{3,2,1,0:T(8,128)(2,1)} %copy-done.1, bf16[2,112,16,128]{3,2,1,0:T(8,128)(2,1)} %pool_ref.5, s32[1792,1]{1,0:T(8,128)} %fusion.5.source_ref, bf16[512,512]{1,0:T(8,128)(2,1)} %all-gather.packed_ref), custom_call_target="tpu_custom_call" | custom-call | tf_op jit(solution)/shard_map/place_pages/pallas_call | solution.py:281
  157.9 27.9 %reduce-scatter.2.cloned.1.call-done = bf16[6,256]{1,0:T(8,128)(2,1)} async-done(((bf16[6,2048]{1,0:T(8,128)(2,1)}), bf16[6,256]{1,0:T(8,128)(2,1)}) %reduce-scatter.2.cloned.1.call-update) | async-done | bytes 3088 | tf_op jit(solution)/shard_map/reduce_scatter | solution.py:263
  (76 shorter events, 11.7 us)
Async XLA Ops:
  7.2 129.1 %copy-start = (bf16[256,2048]{1,0:T(8,128)(2,1)S(1)}, bf16[256,2048]{1,0:T(8,128)(2,1)}, u32[]{:S(2)}) copy-start(bf16[256,2048]{1,0:T(8,128)(2,1)} %param.13) | copy-start | bytes 3145732
  7.2 26.4 %copy-start.2 = (bf16[2048,256]{1,0:T(8,128)(2,1)S(1)}, bf16[2048,256]{1,0:T(8,128)(2,1)}, u32[]{:S(2)}) copy-start(bf16[2048,256]{1,0:T(8,128)(2,1)} %param.11) | copy-start | bytes 3145732
  31.2 0.7 copy-start.7
  32.1 0.7 copy-start.8
  33.4 0.7 copy-start.5
  100.7 24.1 %all-to-all-start = ((f32[64,8,384]{2,1,0:T(8,128)}), f32[64,8,384]{2,1,0:T(8,128)S(1)}, u32[]{:S(2)}, u32[]{:S(2)}) async-start(f32[64,8,384]{2,1,0:T(8,128)} %bitcast.57), calls=%async_computation | async-start | bytes 1572864 | tf_op jit(solution)/shard_map/all_to_all | solution.py:251
  124.8 24.2 %all-to-all-start.1 = ((bf16[128,2,16,128]{3,2,1,0:T(8,128)(2,1)}), bf16[128,2,16,128]{3,2,1,0:T(8,128)(2,1)S(1)}, u32[]{:S(2)}, u32[]{:S(2)}) async-start(bf16[128,2,16,128]{3,2,1,0:T(8,128)(2,1)} %pick_pages.1), calls=%async_computation.2 | async-start | bytes 2097152 | tf_op jit(solution)/shard_map/all_to_all | solution.py:203
  130.2 55.5 %reduce-scatter.2.cloned.1.call-start = ((), (), s32[]{:S(2)}) async-start(), calls=%async_computation.3 | async-start | bytes 36864 | tf_op jit(solution)/shard_map/reduce_scatter | solution.py:263
  131.0 0.7 copy-start.6
  137.8 1.4 copy-start.3
  137.8 1.4 copy-start.4
  149.0 1.0 copy-start.1
Sparse Core Ops, SparseCore 0:
  137.3 48.4 reduce-scatter.1

commit v2 on v1

v2 whole, which is shorter than its diff:
```python
import functools

import jax
import jax.numpy as jnp
from jax import lax
from jax.experimental import pallas as pl
from jax.experimental.pallas import tpu as pltpu
from jax.sharding import PartitionSpec as P

HD = 128
STEPS = 4
PADDED = 8
ROPE_BASE = 1000000.0
NEG_FILL = -1e30
NORM_EPS = 1e-06
VMEM = pltpu.VMEM
SMEM = pltpu.SMEM


def in_vmem():
    return pl.BlockSpec(memory_space=VMEM)


def in_smem():
    return pl.BlockSpec(memory_space=SMEM)


def take(table, index):
    ids = jnp.arange(table.shape[0], dtype=jnp.int32)
    return jnp.sum(jnp.where(index[:, None] == ids[None, :], table[None, :], 0), axis=1)


MESH = pl.DeviceIdType.MESH
EARLY = 24


def remote(source, into, send_sem, recv_sem, **where):
    return pltpu.make_async_remote_copy(
        src_ref=source,
        dst_ref=into,
        send_sem=send_sem,
        recv_sem=recv_sem,
        device_id=where,
        device_id_type=MESH,
    )


def split(value):
    first = value.astype(jnp.bfloat16).astype(jnp.float32)
    rest = value - first
    second = rest.astype(jnp.bfloat16).astype(jnp.float32)
    return first, second, rest - second


def block_kernel(
    pick_ref, tokens_ref, gain_ref, wq_ref, wkv_ref, wout_ref, cos_ref, sin_ref, pool_ref,
    source_ref, owner_ref, pos_ref, req_ref, limit_ref, meta_ref,
    out_ref, arrived_ref, came_ref, fresh_ref,
    tok, pkq, pkkv, queries, fresh_all, keys, values, outgoing, csend, crecv, rsend, rrecv,
    tok_s, tok_r, q1_s, q1_r, q2_s, q2_r, k1_s, k1_r, k2_s, k2_r,
    page_s, page_r, c_s, c_r, r_s, r_r,
):
    me = lax.axis_index("seq")
    tp = lax.axis_index("tp")
    y, z = lax.rem(me, 8), lax.div(me, 8)
    n_seq, n_tp = 64, 8
    slots, page = pool_ref.shape[1], pool_ref.shape[2]

    barrier = pltpu.get_barrier_semaphore()
    for k in range(1, n_tp):
        pl.semaphore_signal(
            barrier, inc=1, device_id={"tp": lax.rem(tp + k, n_tp)}, device_id_type=MESH
        )

    @pl.loop(1, n_seq)
    def _(k):
        pl.semaphore_signal(
            barrier, inc=1, device_id={"seq": lax.rem(me + k, n_seq)}, device_id_type=MESH
        )

    @pl.loop(0, n_seq)
    def _(d):
        for i in range(2):
            s = pick_ref[d * 2 + i]
            outgoing[d, i, 0] = pool_ref[0, s]
            outgoing[d, i, 1] = pool_ref[1, s]

    pl.semaphore_wait(barrier, n_seq - 1 + n_tp - 1)

    def token_copy(k):
        return remote(
            tokens_ref, tok.at[tp], tok_s.at[k], tok_r.at[k], tp=lax.rem(tp + k, n_tp)
        )

    for k in range(1, n_tp):
        token_copy(k).start()
    tok[tp] = tokens_ref[...]

    def page_copy(k):
        d = lax.rem(me + k, n_seq)
        return remote(outgoing.at[d], arrived_ref.at[me], page_s.at[k], page_r.at[k], seq=d)

    @pl.loop(1, 1 + EARLY)
    def _(k):
        page_copy(k).start()

    arrived_ref[me] = outgoing[me]

    for k in range(1, n_tp):
        token_copy(k).wait()

    square = jnp.zeros((PADDED, 1), jnp.float32)
    for i in range(n_tp):
        x = tok[i].astype(jnp.float32)
        square = square + jnp.sum(x * x, axis=1, keepdims=True)
    width = tok.shape[2]
    scale = lax.rsqrt(square / (n_tp * width) + NORM_EPS)
    q = jnp.zeros((PADDED, 2 * HD), jnp.float32)
    kk = jnp.zeros((PADDED, HD), jnp.float32)
    vv = jnp.zeros((PADDED, HD), jnp.float32)
    for i in range(n_tp):
        at = slice(i * width, (i + 1) * width)
        normed = (tok[i].astype(jnp.float32) * scale * gain_ref[i : i + 1, :]).astype(jnp.bfloat16)
        q = q + jnp.dot(normed, wq_ref[at, :], preferred_element_type=jnp.float32)
        kk = kk + jnp.dot(normed, wkv_ref[0, at, :], preferred_element_type=jnp.float32)
        vv = vv + jnp.dot(normed, wkv_ref[1, at, :], preferred_element_type=jnp.float32)

    def turn(x):
        return x * cos_ref[...] + pltpu.roll(x, HD // 2, 1) * sin_ref[...]

    pkq[z, y, :, 0:HD] = turn(q[:, 0:HD]).astype(jnp.bfloat16)
    pkq[z, y, :, HD : 2 * HD] = turn(q[:, HD : 2 * HD]).astype(jnp.bfloat16)
    pkkv[z, y, :, 0:HD] = turn(kk).astype(jnp.bfloat16)
    pkkv[z, y, :, HD : 2 * HD] = vv.astype(jnp.bfloat16)

    def along_y(k):
        return z * 8 + lax.rem(y + k, 8)

    def along_z(k):
        return lax.rem(z + k, 8) * 8 + y

    def q1(k):
        return remote(pkq.at[z, y], pkq.at[z, y], q1_s.at[k], q1_r.at[k], seq=along_y(k))

    def k1(k):
        return remote(pkkv.at[z, y], pkkv.at[z, y], k1_s.at[k], k1_r.at[k], seq=along_z(k))

    def q2(k):
        return remote(pkq.at[z], pkq.at[z], q2_s.at[k], q2_r.at[k], seq=along_z(k))

    def k2(k):
        return remote(pkkv.at[:, y], pkkv.at[:, y], k2_s.at[k], k2_r.at[k], seq=along_y(k))

    for k in range(1, 8):
        q1(k).start()
        k1(k).start()
    for k in range(1, 8):
        q1(k).wait()
    for k in range(1, 8):
        q2(k).start()
    for k in range(1, 8):
        k1(k).wait()
    for k in range(1, 8):
        k2(k).start()

    @pl.loop(1 + EARLY, n_seq)
    def _(k):
        page_copy(k).start()

    for k in range(1, 8):
        k2(k).wait()
    fresh = pkkv[...].astype(jnp.float32).reshape(n_seq * PADDED, 2 * HD)
    fresh_ref[...] = fresh.reshape(n_seq, PADDED, 2 * HD)
    fresh_all[...] = fresh.astype(jnp.bfloat16)

    chunk_slots = 16
    chunk = chunk_slots * page

    @pl.loop(0, slots // chunk_slots)
    def _(c):
        at = pl.ds(pl.multiple_of(c * chunk, chunk), chunk)
        source = source_ref[at, :]
        ids = lax.broadcasted_iota(jnp.int32, (chunk, n_seq * PADDED), 1)
        hot = jnp.where(ids == source, 1.0, 0.0).astype(jnp.bfloat16)
        new = jnp.dot(hot, fresh_all[...], preferred_element_type=jnp.float32)
        for half, into in ((0, keys), (1, values)):
            base = pool_ref[half, pl.ds(c * chunk_slots, chunk_slots)].reshape(chunk, HD)
            into[at, :] = jnp.where(
                source >= 0, new[:, half * HD : (half + 1) * HD], base.astype(jnp.float32)
            ).astype(jnp.bfloat16)

    for k in range(1, 8):
        q2(k).wait()
    queries[...] = (
        pkq[...].astype(jnp.float32).reshape(n_seq * PADDED, 2 * HD).astype(jnp.bfloat16)
    )

    def part_copy(d):
        return remote(csend.at[d], crecv.at[me], c_s.at[d], c_r.at[me], seq=d)

    block = 64

    @pl.loop(0, 8)
    def _(i):
        b = lax.rem(z + i, 8)
        at = pl.ds(pl.multiple_of(b * block, block), block)
        dests = pl.ds(b * 8, 8)
        visible = (owner_ref[...] == req_ref[at, :]) & (pos_ref[...] <= limit_ref[at, :])
        lane = lax.broadcasted_iota(jnp.int32, (block, HD), 1)
        stats = meta_ref[dests].reshape(block, HD)
        for g in range(2):
            query = queries[at, g * HD : (g + 1) * HD]
            scores = lax.dot_general(
                query, keys[...], (((1,), (1,)), ((), ())), preferred_element_type=jnp.float32
            ) * HD ** (-0.5)
            scores = jnp.where(visible, scores, NEG_FILL)
            top = jnp.max(scores, axis=1, keepdims=True)
            some = jnp.where(top > 0.5 * NEG_FILL, 1.0, 0.0)
            weights = jnp.exp(scores - top)
            total = jnp.sum(weights, axis=1, keepdims=True) * some
            part = some * jnp.dot(
                weights.astype(jnp.bfloat16), values[...], preferred_element_type=jnp.float32
            )
            csend[dests, :, g * HD : (g + 1) * HD] = part.reshape(8, PADDED, HD).astype(jnp.bfloat16)
            for j, piece in enumerate(split(top) + split(total)):
                stats = jnp.where(lane == 6 * g + j, piece, stats)
        csend[dests, :, 2 * HD : 3 * HD] = stats.reshape(8, PADDED, HD).astype(jnp.bfloat16)

        @pl.loop(0, 8)
        def _(j):
            d = b * 8 + j

            @pl.when(d != me)
            def _():
                part_copy(d).start()

    crecv[me] = csend[me]

    @pl.loop(0, n_seq)
    def _(d):
        @pl.when(d != me)
        def _():
            remote(csend.at[d], crecv.at[d], c_s.at[d], c_r.at[d], seq=d).wait()

    stats = crecv[:, :, 2 * HD : 3 * HD].astype(jnp.float32)
    came_ref[...] = stats
    mixed = []
    for g in range(2):
        def piece(j):
            return stats[:, :, j : j + 1] + stats[:, :, j + 1 : j + 2] + stats[:, :, j + 2 : j + 3]

        top = piece(6 * g)
        peak = jnp.max(top, axis=0, keepdims=True)
        rescale = jnp.exp(top - peak)
        total = jnp.sum(piece(6 * g + 3) * rescale, axis=0)
        part = crecv[:, :, g * HD : (g + 1) * HD].astype(jnp.float32)
        summed = jnp.sum(part * rescale, axis=0)
        total = jnp.where(total > 0.0, total, 1.0)
        mixed.append((summed / total).astype(jnp.bfloat16))
    attended = jnp.concatenate(mixed, axis=1)

    def sum_copy(k):
        to = lax.rem(tp + k, n_tp)
        return remote(rsend.at[to], rrecv.at[tp], r_s.at[k], r_r.at[k], tp=to)

    for i in range(n_tp):
        rsend[i] = jnp.dot(
            attended, wout_ref[:, i * width : (i + 1) * width], preferred_element_type=jnp.float32
        ).astype(jnp.bfloat16)
    for k in range(1, n_tp):
        sum_copy(k).start()
    rrecv[tp] = rsend[tp]
    for k in range(1, n_tp):
        sum_copy(k).wait()
    result = jnp.zeros((PADDED, width), jnp.float32)
    for i in range(n_tp):
        result = result + rrecv[i].astype(jnp.float32)
    out_ref[...] = result.astype(jnp.bfloat16)

    @pl.loop(1, n_seq)
    def _(k):
        page_copy(k).wait()


def place_kernel(from_ref, req_ref, start_ref, arrived_ref, pool_ref, fresh_ref, out_ref):
    slots, page = pool_ref.shape[1], pool_ref.shape[2]

    @pl.loop(0, slots)
    def _(g):
        s = from_ref[g]

        @pl.when(s >= 0)
        def _():
            out_ref[0, g] = arrived_ref[s, 0]
            out_ref[1, g] = arrived_ref[s, 1]

        @pl.when(s == -1)
        def _():
            out_ref[0, g] = pool_ref[0, g]
            out_ref[1, g] = pool_ref[1, g]

        @pl.when(s < -1)
        def _():
            out_ref[0, g] = jnp.zeros((page, HD), out_ref.dtype)
            out_ref[1, g] = jnp.zeros((page, HD), out_ref.dtype)

        start = start_ref[g]

        @pl.when((start > -STEPS) & (start < page))
        def _():
            ids = lax.broadcasted_iota(jnp.int32, (page, HD), 0)
            both = [out_ref[c, g].astype(jnp.float32) for c in range(2)]
            for t in range(STEPS):
                row = req_ref[g] * STEPS + t
                block = fresh_ref[lax.div(row, 6)]
                line = lax.broadcasted_iota(jnp.int32, block.shape, 0) == lax.rem(row, 6)
                entry = jnp.sum(jnp.where(line, block, 0.0), axis=0, keepdims=True)
                for c in range(2):
                    new = entry[:, c * HD : (c + 1) * HD]
                    both[c] = jnp.where(ids == start + t, new, both[c])
            for c in range(2):
                out_ref[c, g] = both[c].astype(out_ref.dtype)


def local(tokens, norm_gain, w_query, w_key_value, w_out, kv_pool, slot_owner, slot_dest, lengths):
    seq_count = lax.axis_size("seq")
    tp_count = lax.axis_size("tp")
    my_index = lax.axis_index("seq")
    own_rows = tokens.shape[0]
    width = tokens.shape[1]
    slot_count = kv_pool.shape[1]
    page_size = kv_pool.shape[2]
    entries = slot_count * page_size
    capacity = -(-slot_count // seq_count)
    i32 = jnp.int32
    f32 = jnp.float32
    bf16 = jnp.bfloat16

    moving = slot_dest >= 0
    target_dev = jnp.where(moving, slot_dest // slot_count, -1)
    slot_ids = jnp.arange(slot_count, dtype=i32)
    same = (target_dev[None, :] == target_dev[:, None]) & (slot_ids[None, :] < slot_ids[:, None])
    send_rank = jnp.sum(same.astype(i32), axis=1)
    buffer_slot = jnp.where(moving, target_dev * capacity + send_rank, -1)
    hot = buffer_slot[None, :] == jnp.arange(seq_count * capacity, dtype=i32)[:, None]
    filled = jnp.any(hot, axis=1)

    def picked(values):
        return jnp.sum(jnp.where(hot, values[None, :], 0), axis=1)

    pick_slot = picked(slot_ids)
    owner_req = slot_owner[:, 0]
    owner_page = slot_owner[:, 1]
    sent_page = picked(owner_page)
    meta = jnp.stack(
        [
            jnp.where(filled, picked(slot_dest % slot_count), -1),
            picked(owner_req),
            sent_page // 128,
            sent_page % 128,
        ],
        axis=1,
    ).astype(f32)
    meta = meta.reshape(seq_count, 1, capacity * 4)
    meta = jnp.pad(meta, ((0, 0), (0, 0), (12, HD - 12 - capacity * 4)))
    meta = jnp.broadcast_to(meta, (seq_count, PADDED, HD))

    own_index = my_index * own_rows + jnp.arange(PADDED, dtype=i32)
    own_positions = take(lengths, own_index // STEPS) + own_index % STEPS
    frequency = ROPE_BASE ** (-jnp.arange(HD // 2, dtype=f32) * 2.0 / HD)
    angles = own_positions.astype(f32)[:, None] * frequency[None, :]
    cosine, sine = jnp.cos(angles), jnp.sin(angles)
    cosine = jnp.concatenate([cosine, cosine], axis=1)
    sine = jnp.concatenate([-sine, sine], axis=1)

    padded_ids = jnp.arange(seq_count * PADDED, dtype=i32)
    row_of = padded_ids // PADDED * own_rows + padded_ids % PADDED
    real = padded_ids % PADDED < own_rows
    row_req = jnp.where(real, row_of // STEPS, -2)
    row_limit = take(lengths, row_req) + row_of % STEPS
    base_len = take(lengths, owner_req)
    offset = jnp.arange(page_size, dtype=i32)
    position = owner_page[:, None] * page_size + offset[None, :]
    step_of = position - base_len[:, None]
    is_new = (owner_req >= 0)[:, None] & (step_of >= 0) & (step_of < STEPS)
    row = owner_req[:, None] * STEPS + step_of
    source = jnp.where(is_new, row // own_rows * PADDED + row % own_rows, -1)
    entry_owner = jnp.broadcast_to(owner_req[:, None], (slot_count, page_size))

    rows = seq_count * PADDED
    page_shape = (seq_count, capacity, 2, page_size, HD)
    dma = pltpu.SemaphoreType.DMA
    attn_out, arrived, came, fresh = pl.pallas_call(
        block_kernel,
        out_shape=[
            jax.ShapeDtypeStruct((PADDED, width), bf16),
            jax.ShapeDtypeStruct(page_shape, bf16),
            jax.ShapeDtypeStruct((seq_count, PADDED, HD), f32),
            jax.ShapeDtypeStruct((seq_count, PADDED, 2 * HD), f32),
        ],
        in_specs=[in_smem()] + [in_vmem()] * 14,
        out_specs=[in_vmem()] * 4,
        scratch_shapes=[
            VMEM((tp_count, PADDED, width), bf16),
            VMEM((8, 8, PADDED, 2 * HD), bf16),
            VMEM((8, 8, PADDED, 2 * HD), bf16),
            VMEM((rows, 2 * HD), bf16),
            VMEM((rows, 2 * HD), bf16),
            VMEM((entries, HD), bf16),
            VMEM((entries, HD), bf16),
            VMEM(page_shape, bf16),
            VMEM((seq_count, PADDED, 3 * HD), bf16),
            VMEM((seq_count, PADDED, 3 * HD), bf16),
            VMEM((tp_count, PADDED, width), bf16),
            VMEM((tp_count, PADDED, width), bf16),
        ]
        + [dma((8,))] * 10
        + [dma((seq_count,))] * 4
        + [dma((8,))] * 2,
        compiler_params=pltpu.CompilerParams(collective_id=0, has_side_effects=True),
        name="block",
    )(
        pick_slot,
        jnp.pad(tokens, ((0, PADDED - own_rows), (0, 0))),
        norm_gain.reshape(tp_count, width),
        w_query,
        w_key_value,
        w_out,
        cosine,
        sine,
        kv_pool,
        source.reshape(entries, 1),
        entry_owner.reshape(1, entries),
        position.reshape(1, entries),
        row_req[:, None],
        row_limit[:, None],
        meta,
    )

    came = came[:, 0, 12 : 12 + capacity * 4].astype(i32).reshape(seq_count * capacity, 4)
    lands = came[None, :, 0] == slot_ids[:, None]
    landed = jnp.any(lands, axis=1)

    def landing(values):
        return jnp.sum(jnp.where(lands, values[None, :], 0), axis=1)

    from_index = jnp.where(
        landed,
        landing(jnp.arange(seq_count * capacity, dtype=i32)),
        jnp.where(moving, -2, -1),
    )
    came_req = came[:, 1]
    came_start = take(lengths, came_req) - (came[:, 2] * 128 + came[:, 3]) * page_size
    own_start = jnp.where(
        (owner_req < 0) | moving, page_size, base_len - owner_page * page_size
    )
    final_req = jnp.where(landed, landing(came_req), owner_req)
    final_start = jnp.where(landed, landing(came_start), own_start)
    kv_moved = pl.pallas_call(
        place_kernel,
        out_shape=jax.ShapeDtypeStruct(kv_pool.shape, kv_pool.dtype),
        in_specs=[in_smem()] * 3 + [in_vmem()] * 3,
        out_specs=in_vmem(),
        name="place_pages",
    )(
        from_index,
        final_req,
        final_start,
        arrived.reshape(seq_count * capacity, 2, page_size, HD),
        kv_pool,
        fresh,
    )
    return (attn_out[:own_rows], kv_moved)


def solution(mesh):
    in_specs = (
        P("seq", "tp"),
        P(),
        P(None, "tp"),
        P(None, None, "tp"),
        P("tp", None),
        P(None, "seq", None, "tp"),
        P("seq", None),
        P("seq"),
        P(),
    )
    out_specs = (P("seq", "tp"), P(None, "seq", None, "tp"))
    return jax.shard_map(local, mesh=mesh, in_specs=in_specs, out_specs=out_specs, check_vma=False)
```

time: 194 us -> 114 us (0.59)
  Pallas kernels: 24.6 us -> 95.8 us
  blocking collectives: 63.8 us -> 0 us
  waiting for transfers between devices: 48.6 us -> 0 us
  between operations: 14.3 us -> 0.8 us
  starting transfers between devices: 13 us -> 0 us
  local copies, waits for them, and re-layouts: 13.6 us -> 9.5 us
  matrix products: 3.76 us -> 0 us
  other arithmetic: 10.9 us -> 7.21 us
    pallas_call x2 -> x1, Pallas kernels: 16.8 us -> 89.6 us  [local(): pl.pallas_call(block_kernel, out_shape=[jax.ShapeDtypeStruct((PADDED, wid...]
    all_gather x2 -> x0, blocking collectives: 63.8 us -> none  [the longest x1 44.1 us: local(): packed = lax.all_gather(own_packed[None], 'seq', axis=0, tiled=True)]
    reduce_scatter x1 -> x0, waiting for transfers between devices: 27.9 us -> none  [local(): lax.psum_scatter(partial_out[:own_rows].astype(jnp.bfloat16), 'tp', scatt...]
    all_to_all x2 -> x0, waiting for transfers between devices: 20.7 us -> none  [the longest x1 13.6 us: local(): lax.all_to_all(partials.reshape(seq_count, PADDED, 3 * HD), 'seq', split_...]
    all_to_all x2 -> x0, starting transfers between devices: 13 us -> none  [the longest x1 7.5 us: local(): lax.all_to_all(partials.reshape(seq_count, PADDED, 3 * HD), 'seq', split_...]
    dot_general x4 -> x0, matrix products: 3.76 us -> none  [the longest x1 1.3 us: project_rows(): keys = jnp.dot(normed, w_key_value[0], preferred_element_type=jnp.float32)]
    select_n x4, other arithmetic: 4.16 us -> 2.08 us  [the longest x1 1.46 us: local(): source = jnp.where(is_new, row // own_rows * PADDED + row % own_rows, -1)]
    unnamed x22 -> x15, local copies, waits for them, and re-layouts: 4 us -> 3.35 us
  transfers between devices with their start and end apart: 3 -> 0, of which waited for: 3 -> 0; matrix products, arithmetic and copies ran while one was open for 6% -> 0% of each run, Pallas kernels for 6% -> 0%
where the time goes in v2:
time: 114 us; the launch traced here: 113 us
  Pallas kernels  95.8 us (84%)
  local copies, waits for them, and re-layouts  9.5 us (8%)
  other arithmetic  7.21 us (6%)
    pallas_call x1, Pallas kernels, local(): pl.pallas_call(block_kernel, out_shape=[jax.ShapeDtypeStruct((PADDED, wid...  89.6 us
    pallas_call x1, Pallas kernels, local(): pl.pallas_call(place_kernel, out_shape=jax.ShapeDtypeStruct(kv_pool.shape...  6.24 us
    unnamed x15, local copies, waits for them, and re-layouts  3.35 us

profile of v2, /device:TPU:1, one launch (start us, length us, event | category | flops | bytes accessed | tf_op | source)
XLA Modules:
  0.0 113.3 jit_solution(13881171619685009355)
XLA Ops:
  0.6 0.7 copy-done.3
  1.3 0.6 copy-done.4
  2.2 0.6 copy-done.5
  2.8 0.2 select_reduce_fusion.10
  3.4 0.7 select_reduce_fusion.6
  4.2 0.6 copy-done.1
  4.8 0.6 pad.8.tokens_ref
  5.4 0.6 reshape.466.gain_ref
  6.1 0.7 pad_maximum_fusion
  7.0 0.7 reshape.467.owner_ref
  8.1 0.7 add.260.pos_ref
  8.8 0.6 reshape.473
  9.3 0.7 broadcast_in_dim.191.meta_ref
  10.1 0.6 reshape.472
  10.8 1.1 fusion.11
  11.9 0.5 rem.197
  12.4 0.5 div.109
  12.9 1.5 %fusion.2.source_ref = s32[1792,1]{1,0:T(8,128)} fusion(pred[1792,1]{1,0:T(8,128)(4,1)S(1)} %reshape.472, s32[1792,1]{1,0:T(8,128)S(1)} %div.109, s32[1792,1]{1,0:T(8,128)S(1)} %rem.197, pred[1792,1]{1,0:T(8,128)(4,1)S(1)} %reshape.473), kind=kLoop, calls=%fused_computation.4 | loop fusion | flops 19712 | bytes 25088 | tf_op jit(solution)/shard_map/jit(_where)/select_n | solution.py:387
  14.4 89.6 %block.1 = (bf16[8,256]{1,0:T(8,128)(2,1)}, bf16[64,2,2,16,128]{4,3,2,1,0:T(8,128)(2,1)}, f32[64,8,128]{2,1,0:T(8,128)}, f32[64,8,256]{2,1,0:T(8,128)}) custom-call(s32[128]{0:T(128)} %get-tuple-element.18.pick_ref, bf16[8,256]{1,0:T(8,128)(2,1)} %pad.8.tokens_ref, f32[8,256]{1,0:T(8,128)} %reshape.466.gain_ref, bf16[2048,256]{1,0:T(8,128)(2,1)} %wq_ref.1, ...), custom_call_target="tpu_custom_call" | custom-call | tf_op jit(solution)/shard_map/block/pallas_call | solution.py:393
  104.0 1.1 convert_reduce_fusion.1
  105.2 0.2 fusion.39
  105.9 0.6 fusion.35
  106.5 6.2 %place_pages.1 = bf16[2,112,16,128]{3,2,1,0:T(8,128)(2,1)} custom-call(s32[112]{0:T(128)} %get-tuple-element.27.from_ref, s32[112]{0:T(128)} %get-tuple-element.24.req_ref, s32[112]{0:T(128)} %get-tuple-element.23.start_ref, bf16[128,2,16,128]{3,2,1,0:T(8,128)(2,1)} %bitcast.41, bf16[2,112,16,128]{3,2,1,0:T(8,128)(2,1)} %pool_ref.3, ...), custom_call_target="tpu_custom_call" | custom-call | tf_op jit(solution)/shard_map/place_pages/pallas_call | solution.py:459
  112.7 0.6 copy.54
  (38 shorter events, 2.1 us)
Async XLA Ops:
  0.6 0.7 copy-start.3
  1.3 0.7 copy-start.4
  2.2 0.7 copy-start.5
  4.1 0.7 copy-start.1
  4.1 1.3 %copy-start = (f32[2048]{0:T(1024)S(1)}, f32[2048]{0:T(1024)}, u32[]{:S(2)}) copy-start(f32[2048]{0:T(1024)} %param.10) | copy-start | bytes 24580
  106.5 6.2 %copy-start.2 = (bf16[8,256]{1,0:T(8,128)(2,1)S(1)}, bf16[8,256]{1,0:T(8,128)(2,1)}, u32[]{:S(2)}) copy-start(bf16[8,256]{1,0:T(8,128)(2,1)} %get-tuple-element.6) | copy-start | bytes 12292

commit v3 on v2

--- a/solution.py
+++ b/solution.py
@@ -52,10 +52,97 @@
     return first, second, rest - second
 
 
+def iota(shape, dim):
+    return lax.broadcasted_iota(jnp.int32, shape, dim)
+
+
+def ones_where(mask):
+    return jnp.where(mask, 1.0, 0.0)
+
+
+def prepare(
+    owner_ref, dest_ref, lengths_ref, hot, entry_owner, entry_pos, req_ref, limit_ref, meta_ref,
+    n_seq, slots, page, own_rows,
+):
+    f32, bf16 = jnp.float32, jnp.bfloat16
+    rows, entries = n_seq * PADDED, slots * page
+    across = (((1,), (1,)), ((), ()))
+    owner = owner_ref[...].astype(f32)
+    req, number = owner[0:1, :], owner[1:2, :]
+    high = jnp.floor(number * (1.0 / 128))
+    low = number - high * 128.0
+    line = iota((HD, slots), 0)
+    parts = jnp.where(line == 0, req, jnp.where(line == 1, high, jnp.where(line == 2, low, 0.0)))
+    parts = parts.astype(bf16)
+
+    spread = ones_where(
+        lax.shift_right_logical(iota((slots, entries), 1), 4) == iota((slots, entries), 0)
+    ).astype(bf16)
+    wide = jnp.dot(parts[0:16, :], spread, preferred_element_type=f32)
+    entry_owner[...] = wide[0:1, :]
+    inner = (iota((1, entries), 1) & (page - 1)).astype(f32)
+    entry_pos[...] = (wide[1:2, :] * 128.0 + wide[2:3, :]) * page + inner
+
+    def row_facts(ids):
+        j = ids & (PADDED - 1)
+        row = lax.shift_right_logical(ids, 3) * own_rows + j
+        wanted = jnp.where(j < own_rows, lax.shift_right_logical(row, 2), -2)
+        return wanted.astype(f32), (row & (STEPS - 1)).astype(f32)
+
+    lengths = lengths_ref[...].astype(f32)
+    count = lengths.shape[1]
+    wanted, step = row_facts(iota((rows, 1), 0))
+    match = iota((rows, count), 1).astype(f32) == wanted
+    req_ref[...] = wanted
+    limit_ref[...] = step + jnp.sum(jnp.where(match, lengths, 0.0), axis=1, keepdims=True)
+    eye = iota((count, count), 0) == iota((count, count), 1)
+    length_col = jnp.sum(jnp.where(eye, lengths, 0.0), axis=1, keepdims=True)
+    wanted_row, step_row = row_facts(iota((1, rows), 1))
+    match = iota((count, rows), 0).astype(f32) == wanted_row
+    limit_row = step_row + jnp.sum(jnp.where(match, length_col, 0.0), axis=0, keepdims=True)
+
+    chunk = 16 * page
+
+    @pl.loop(0, entries // chunk)
+    def _(c):
+        slot = lax.shift_right_logical(iota((chunk, slots), 0), 4) + c * 16
+        near = ones_where(slot == iota((chunk, slots), 1)).astype(bf16)
+        tall = lax.dot_general(near, parts, across, preferred_element_type=f32)
+        at_inner = (iota((chunk, 1), 0) & (page - 1)).astype(f32)
+        place = (tall[:, 1:2] * 128.0 + tall[:, 2:3]) * page + at_inner
+        mask = (tall[:, 0:1] == wanted_row) & (place == limit_row)
+        hot[pl.ds(pl.multiple_of(c * chunk, chunk), chunk), :] = ones_where(mask).astype(bf16)
+
+    dest = dest_ref[...].astype(f32)
+    device = jnp.floor((dest + 0.5) * (1.0 / slots))
+    landing = dest - device * slots
+    ahead, behind = iota((slots, slots), 0), iota((slots, slots), 1)
+    device_col = jnp.sum(jnp.where(ahead == behind, device, 0.0), axis=1, keepdims=True)
+    rank = jnp.sum(
+        ones_where((device_col == device) & (ahead < behind)), axis=0, keepdims=True
+    )
+    place = jnp.where(dest >= 0.0, device * 2.0 + rank, -1.0)
+    ids = iota((rows, slots), 0)
+    j = ids & (PADDED - 1)
+    wants = jnp.where(j < 2, lax.shift_right_logical(ids, 3) * 2 + j, -2).astype(f32)
+    facts = jnp.where(
+        line == 12,
+        landing + 1.0,
+        jnp.where(line == 13, req, jnp.where(line == 14, high, jnp.where(line == 15, low, 0.0))),
+    )
+    meta_ref[...] = lax.dot_general(
+        ones_where(wants == place).astype(bf16),
+        facts.astype(bf16),
+        across,
+        preferred_element_type=f32,
+    )
+
+
 def block_kernel(
     pick_ref, tokens_ref, gain_ref, wq_ref, wkv_ref, wout_ref, cos_ref, sin_ref, pool_ref,
-    source_ref, owner_ref, pos_ref, req_ref, limit_ref, meta_ref,
+    owner_ref, dest_ref, lengths_ref,
     out_ref, arrived_ref, came_ref, fresh_ref,
+    tsend, hot, entry_owner, entry_pos, req_ref, limit_ref, meta_ref,
     tok, pkq, pkkv, queries, fresh_all, keys, values, outgoing, csend, crecv, rsend, rrecv,
     tok_s, tok_r, q1_s, q1_r, q2_s, q2_r, k1_s, k1_r, k2_s, k2_r,
     page_s, page_r, c_s, c_r, r_s, r_r,
@@ -78,6 +165,9 @@
             barrier, inc=1, device_id={"seq": lax.rem(me + k, n_seq)}, device_id_type=MESH
         )
 
+    tsend[...] = jnp.zeros_like(tsend)
+    tsend[0 : tokens_ref.shape[0], :] = tokens_ref[...]
+
     @pl.loop(0, n_seq)
     def _(d):
         for i in range(2):
@@ -85,19 +175,24 @@
             outgoing[d, i, 0] = pool_ref[0, s]
             outgoing[d, i, 1] = pool_ref[1, s]
 
+    prepare(
+        owner_ref, dest_ref, lengths_ref, hot, entry_owner, entry_pos, req_ref, limit_ref,
+        meta_ref, n_seq, slots, page, tokens_ref.shape[0],
+    )
     pl.semaphore_wait(barrier, n_seq - 1 + n_tp - 1)
 
     def token_copy(k):
         return remote(
-            tokens_ref, tok.at[tp], tok_s.at[k], tok_r.at[k], tp=lax.rem(tp + k, n_tp)
+            tsend, tok.at[tp], tok_s.at[k], tok_r.at[k], tp=lax.rem(tp + k, n_tp)
         )
 
     for k in range(1, n_tp):
         token_copy(k).start()
-    tok[tp] = tokens_ref[...]
+    tok[tp] = tsend[...]
 
     def page_copy(k):
-        d = lax.rem(me + k, n_seq)
+        turn_by = lax.rem(k * 27, n_seq)
+        d = lax.rem(z + lax.div(turn_by, 8), 8) * 8 + lax.rem(y + lax.rem(turn_by, 8), 8)
         return remote(outgoing.at[d], arrived_ref.at[me], page_s.at[k], page_r.at[k], seq=d)
 
     @pl.loop(1, 1 + EARLY)
@@ -120,7 +215,7 @@
     vv = jnp.zeros((PADDED, HD), jnp.float32)
     for i in range(n_tp):
         at = slice(i * width, (i + 1) * width)
-        normed = (tok[i].astype(jnp.float32) * scale * gain_ref[i : i + 1, :]).astype(jnp.bfloat16)
+        normed = (tok[i].astype(jnp.float32) * scale * gain_ref[:, at]).astype(jnp.bfloat16)
         q = q + jnp.dot(normed, wq_ref[at, :], preferred_element_type=jnp.float32)
         kk = kk + jnp.dot(normed, wkv_ref[0, at, :], preferred_element_type=jnp.float32)
         vv = vv + jnp.dot(normed, wkv_ref[1, at, :], preferred_element_type=jnp.float32)
@@ -171,7 +266,8 @@
         k2(k).wait()
     fresh = pkkv[...].astype(jnp.float32).reshape(n_seq * PADDED, 2 * HD)
     fresh_ref[...] = fresh.reshape(n_seq, PADDED, 2 * HD)
-    fresh_all[...] = fresh.astype(jnp.bfloat16)
+    fresh_all[:, 0 : 2 * HD] = fresh.astype(jnp.bfloat16)
+    fresh_all[:, 2 * HD : 3 * HD] = jnp.ones((n_seq * PADDED, HD), jnp.bfloat16)
 
     chunk_slots = 16
     chunk = chunk_slots * page
@@ -179,14 +275,12 @@
     @pl.loop(0, slots // chunk_slots)
     def _(c):
         at = pl.ds(pl.multiple_of(c * chunk, chunk), chunk)
-        source = source_ref[at, :]
-        ids = lax.broadcasted_iota(jnp.int32, (chunk, n_seq * PADDED), 1)
-        hot = jnp.where(ids == source, 1.0, 0.0).astype(jnp.bfloat16)
-        new = jnp.dot(hot, fresh_all[...], preferred_element_type=jnp.float32)
+        new = jnp.dot(hot[at, :], fresh_all[...], preferred_element_type=jnp.float32)
+        is_new = new[:, 2 * HD : 3 * HD] > 0.5
         for half, into in ((0, keys), (1, values)):
             base = pool_ref[half, pl.ds(c * chunk_slots, chunk_slots)].reshape(chunk, HD)
             into[at, :] = jnp.where(
-                source >= 0, new[:, half * HD : (half + 1) * HD], base.astype(jnp.float32)
+                is_new, new[:, half * HD : (half + 1) * HD], base.astype(jnp.float32)
             ).astype(jnp.bfloat16)
 
     for k in range(1, 8):
@@ -202,12 +296,13 @@
 
     @pl.loop(0, 8)
     def _(i):
-        b = lax.rem(z + i, 8)
+        away = lax.div(i + 1, 2)
+        b = lax.rem(z + jnp.where(lax.rem(i, 2) == 1, away, 8 - away), 8)
         at = pl.ds(pl.multiple_of(b * block, block), block)
         dests = pl.ds(b * 8, 8)
-        visible = (owner_ref[...] == req_ref[at, :]) & (pos_ref[...] <= limit_ref[at, :])
+        visible = (entry_owner[...] == req_ref[at, :]) & (entry_pos[...] <= limit_ref[at, :])
         lane = lax.broadcasted_iota(jnp.int32, (block, HD), 1)
-        stats = meta_ref[dests].reshape(block, HD)
+        stats = meta_ref[at, :]
         for g in range(2):
             query = queries[at, g * HD : (g + 1) * HD]
             scores = lax.dot_general(
@@ -275,7 +370,7 @@
     result = jnp.zeros((PADDED, width), jnp.float32)
     for i in range(n_tp):
         result = result + rrecv[i].astype(jnp.float32)
-    out_ref[...] = result.astype(jnp.bfloat16)
+    out_ref[...] = result[0 : out_ref.shape[0], :].astype(jnp.bfloat16)
 
     @pl.loop(1, n_seq)
     def _(k):
@@ -343,7 +438,6 @@
     send_rank = jnp.sum(same.astype(i32), axis=1)
     buffer_slot = jnp.where(moving, target_dev * capacity + send_rank, -1)
     hot = buffer_slot[None, :] == jnp.arange(seq_count * capacity, dtype=i32)[:, None]
-    filled = jnp.any(hot, axis=1)
 
     def picked(values):
         return jnp.sum(jnp.where(hot, values[None, :], 0), axis=1)
@@ -351,19 +445,7 @@
     pick_slot = picked(slot_ids)
     owner_req = slot_owner[:, 0]
     owner_page = slot_owner[:, 1]
-    sent_page = picked(owner_page)
-    meta = jnp.stack(
-        [
-            jnp.where(filled, picked(slot_dest % slot_count), -1),
-            picked(owner_req),
-            sent_page // 128,
-            sent_page % 128,
-        ],
-        axis=1,
-    ).astype(f32)
-    meta = meta.reshape(seq_count, 1, capacity * 4)
-    meta = jnp.pad(meta, ((0, 0), (0, 0), (12, HD - 12 - capacity * 4)))
-    meta = jnp.broadcast_to(meta, (seq_count, PADDED, HD))
+    base_len = take(lengths, owner_req)
 
     own_index = my_index * own_rows + jnp.arange(PADDED, dtype=i32)
     own_positions = take(lengths, own_index // STEPS) + own_index % STEPS
@@ -373,39 +455,32 @@
     cosine = jnp.concatenate([cosine, cosine], axis=1)
     sine = jnp.concatenate([-sine, sine], axis=1)
 
-    padded_ids = jnp.arange(seq_count * PADDED, dtype=i32)
-    row_of = padded_ids // PADDED * own_rows + padded_ids % PADDED
-    real = padded_ids % PADDED < own_rows
-    row_req = jnp.where(real, row_of // STEPS, -2)
-    row_limit = take(lengths, row_req) + row_of % STEPS
-    base_len = take(lengths, owner_req)
-    offset = jnp.arange(page_size, dtype=i32)
-    position = owner_page[:, None] * page_size + offset[None, :]
-    step_of = position - base_len[:, None]
-    is_new = (owner_req >= 0)[:, None] & (step_of >= 0) & (step_of < STEPS)
-    row = owner_req[:, None] * STEPS + step_of
-    source = jnp.where(is_new, row // own_rows * PADDED + row % own_rows, -1)
-    entry_owner = jnp.broadcast_to(owner_req[:, None], (slot_count, page_size))
-
     rows = seq_count * PADDED
     page_shape = (seq_count, capacity, 2, page_size, HD)
     dma = pltpu.SemaphoreType.DMA
     attn_out, arrived, came, fresh = pl.pallas_call(
         block_kernel,
         out_shape=[
-            jax.ShapeDtypeStruct((PADDED, width), bf16),
+            jax.ShapeDtypeStruct((own_rows, width), bf16),
             jax.ShapeDtypeStruct(page_shape, bf16),
             jax.ShapeDtypeStruct((seq_count, PADDED, HD), f32),
             jax.ShapeDtypeStruct((seq_count, PADDED, 2 * HD), f32),
         ],
-        in_specs=[in_smem()] + [in_vmem()] * 14,
+        in_specs=[in_smem()] + [in_vmem()] * 11,
         out_specs=[in_vmem()] * 4,
         scratch_shapes=[
+            VMEM((PADDED, width), bf16),
+            VMEM((entries, rows), bf16),
+            VMEM((1, entries), f32),
+            VMEM((1, entries), f32),
+            VMEM((rows, 1), f32),
+            VMEM((rows, 1), f32),
+            VMEM((rows, HD), f32),
             VMEM((tp_count, PADDED, width), bf16),
             VMEM((8, 8, PADDED, 2 * HD), bf16),
             VMEM((8, 8, PADDED, 2 * HD), bf16),
             VMEM((rows, 2 * HD), bf16),
-            VMEM((rows, 2 * HD), bf16),
+            VMEM((rows, 3 * HD), bf16),
             VMEM((entries, HD), bf16),
             VMEM((entries, HD), bf16),
             VMEM(page_shape, bf16),
@@ -421,24 +496,21 @@
         name="block",
     )(
         pick_slot,
-        jnp.pad(tokens, ((0, PADDED - own_rows), (0, 0))),
-        norm_gain.reshape(tp_count, width),
+        tokens,
+        norm_gain[None, :],
         w_query,
         w_key_value,
         w_out,
         cosine,
         sine,
         kv_pool,
-        source.reshape(entries, 1),
-        entry_owner.reshape(1, entries),
-        position.reshape(1, entries),
-        row_req[:, None],
-        row_limit[:, None],
-        meta,
-    )
-
-    came = came[:, 0, 12 : 12 + capacity * 4].astype(i32).reshape(seq_count * capacity, 4)
-    lands = came[None, :, 0] == slot_ids[:, None]
+        slot_owner.T,
+        slot_dest[None, :],
+        lengths[None, :],
+    )
+
+    came = came[:, :capacity, 12:16].astype(i32).reshape(seq_count * capacity, 4)
+    lands = came[None, :, 0] - 1 == slot_ids[:, None]
     landed = jnp.any(lands, axis=1)
 
     def landing(values):
@@ -470,7 +542,7 @@
         kv_pool,
         fresh,
     )
-    return (attn_out[:own_rows], kv_moved)
+    return (attn_out, kv_moved)
 
 
 def solution(mesh):

time: 114 us -> 90.8 us (0.80)
  Pallas kernels: 95.8 us -> 81.5 us
  local copies, waits for them, and re-layouts: 9.5 us -> 4.1 us
  other arithmetic: 7.21 us -> 4.19 us
    pallas_call x1, Pallas kernels: 89.6 us -> 75.4 us  [local(): pl.pallas_call(block_kernel, out_shape=[jax.ShapeDtypeStruct((own_rows, w...]
    select_n x5 -> x0, other arithmetic: 2.6 us -> none  [the longest x1 1.46 us: local(): source = jnp.where(is_new, row // own_rows * PADDED + row % own_rows, -1)]
    reshape x2 -> x0, local copies, waits for them, and re-layouts: 1.29 us -> none  [the longest x1 0.7 us: local(): entry_owner.reshape(1, entries)]
    unnamed x15 -> x19, local copies, waits for them, and re-layouts: 3.35 us -> 4.1 us
where the time goes in v3:
time: 90.8 us; the launch traced here: 90.6 us
  Pallas kernels  81.5 us (90%)
  other arithmetic  4.19 us (5%)
  local copies, waits for them, and re-layouts  4.1 us (5%)
    pallas_call x1, Pallas kernels, local(): pl.pallas_call(block_kernel, out_shape=[jax.ShapeDtypeStruct((own_rows, w...  75.4 us
    pallas_call x1, Pallas kernels, local(): pl.pallas_call(place_kernel, out_shape=jax.ShapeDtypeStruct(kv_pool.shape...  6.16 us
    unnamed x19, local copies, waits for them, and re-layouts  4.1 us

profile of v3, /device:TPU:1, one launch (start us, length us, event | category | flops | bytes accessed | tf_op | source)
XLA Modules:
  0.0 90.6 jit_solution(8609313113000374969)
XLA Ops:
  0.6 0.7 copy-done
  1.3 0.7 copy-done.5
  2.0 0.1 select_reduce_fusion.4
  2.1 0.6 copy-done.3
  2.6 0.2 convert_reduce_fusion
  2.8 0.7 select_reduce_fusion.3.pick_ref
  3.5 0.2 select_reduce_fusion.6
  3.8 0.1 fusion.2
  3.9 0.7 pad_maximum_fusion
  4.6 75.4 %block.1 = (bf16[6,256]{1,0:T(8,128)(2,1)}, bf16[64,2,2,16,128]{4,3,2,1,0:T(8,128)(2,1)}, f32[64,8,128]{2,1,0:T(8,128)}, f32[64,8,256]{2,1,0:T(8,128)}) custom-call(s32[128]{0:T(128)} %select_reduce_fusion.3.pick_ref, bf16[6,256]{1,0:T(8,128)(2,1)} %tokens_ref.1, f32[1,2048]{1,0:T(1,128)} %bitcast.22, bf16[2048,256]{1,0:T(8,128)(2,1)} %wq_ref.1, ...), custom_call_target="tpu_custom_call" | custom-call | tf_op jit(solution)/shard_map/block/pallas_call | solution.py:461
  80.0 1.1 %slice_convert_fusion = s32[64,2,4]{2,1,0:T(2,128)S(1)} fusion(f32[64,8,128]{2,1,0:T(8,128)} %get-tuple-element.7), kind=kLoop, calls=%fused_computation.1 | loop fusion | flops 512 | bytes 4096 | tf_op jit(solution)/shard_map/convert_element_type | solution.py:512
  81.0 0.1 fusion.8
  81.2 0.1 copy.21
  81.2 0.1 copy.20
  81.3 0.7 copy-done.6
  82.0 0.1 select_reduce_fusion.5
  82.1 0.1 copy.23
  82.1 0.1 fusion
  82.3 0.1 copy.22
  82.3 0.2 select_reduce_fusion
  82.5 0.7 copy-done.1
  83.2 0.6 fusion.4
  83.8 6.2 %place_pages.1 = bf16[2,112,16,128]{3,2,1,0:T(8,128)(2,1)} custom-call(s32[112]{0:T(128)} %get-tuple-element.19.from_ref, s32[112]{0:T(128)} %get-tuple-element.18.req_ref, s32[112]{0:T(128)} %get-tuple-element.17.start_ref, bf16[128,2,16,128]{3,2,1,0:T(8,128)(2,1)} %bitcast.21, bf16[2,112,16,128]{3,2,1,0:T(8,128)(2,1)} %pool_ref.3, ...), custom_call_target="tpu_custom_call" | custom-call | tf_op jit(solution)/shard_map/place_pages/pallas_call | solution.py:531
  90.0 0.6 copy.25
  (16 shorter events, 0.1 us)
Async XLA Ops:
  0.6 0.7 copy-start
  1.3 0.7 copy-start.5
  2.0 0.7 copy-start.3
  81.3 0.7 copy-start.6
  82.5 0.7 copy-start.1
  82.5 0.7 copy-start.4
  83.8 6.2 %copy-start.2 = (bf16[6,256]{1,0:T(8,128)(2,1)S(1)}, bf16[6,256]{1,0:T(8,128)(2,1)}, u32[]{:S(2)}) copy-start(bf16[6,256]{1,0:T(8,128)(2,1)} %get-tuple-element.27) | copy-start | bytes 9220

commit v4 on v3

--- a/solution.py
+++ b/solution.py
@@ -31,7 +31,7 @@
 
 
 MESH = pl.DeviceIdType.MESH
-EARLY = 24
+EARLY = 8
 
 
 def remote(source, into, send_sem, recv_sem, **where):
@@ -138,11 +138,42 @@
     )
 
 
+def plan(stats, owner_ref, dest_ref, lengths_ref, plan_ref, n_seq, slots, page):
+    f32 = jnp.float32
+    rows = n_seq * PADDED
+    ids = iota((rows, slots), 0)
+    j = ids & (PADDED - 1)
+    index = (lax.shift_right_logical(ids, 3) * 2 + j).astype(f32)
+    lands = (j < 2) & (stats[:, 12:13] == (iota((rows, slots), 1) + 1).astype(f32))
+
+    def landing(value):
+        return jnp.sum(jnp.where(lands, value, 0.0), axis=0, keepdims=True)
+
+    landed = landing(jnp.ones((rows, slots), f32)) > 0.5
+    moving = dest_ref[...].astype(f32) >= 0.0
+    owner = owner_ref[...].astype(f32)
+    stay = jnp.where(moving, -1.0, owner[0:1, :])
+    req = jnp.where(landed, landing(stats[:, 13:14]), stay)
+    number = landing(stats[:, 14:15]) * 128.0 + landing(stats[:, 15:16])
+    number = jnp.where(landed, number, owner[1:2, :])
+    lengths = lengths_ref[...].astype(f32)
+    count = lengths.shape[1]
+    eye = iota((count, count), 0) == iota((count, count), 1)
+    length_col = jnp.sum(jnp.where(eye, lengths, 0.0), axis=1, keepdims=True)
+    match = iota((count, slots), 0).astype(f32) == req
+    base = jnp.sum(jnp.where(match, length_col, 0.0), axis=0, keepdims=True)
+    start = jnp.where(req >= 0.0, base - number * page, float(page))
+    source = jnp.where(landed, landing(index), jnp.where(moving, -2.0, -1.0))
+    line = iota((8, slots), 0)
+    table = jnp.where(line == 0, source, jnp.where(line == 1, req, start))
+    plan_ref[...] = table.astype(jnp.int32)
+
+
 def block_kernel(
-    pick_ref, tokens_ref, gain_ref, wq_ref, wkv_ref, wout_ref, cos_ref, sin_ref, pool_ref,
+    pick_ref, tokens_ref, gain_ref, wq_hbm, wkv_hbm, wout_hbm, cos_ref, sin_ref, pool_ref,
     owner_ref, dest_ref, lengths_ref,
-    out_ref, arrived_ref, came_ref, fresh_ref,
-    tsend, hot, entry_owner, entry_pos, req_ref, limit_ref, meta_ref,
+    out_ref, arrived_ref, plan_ref, fresh_ref,
+    wq_ref, wkv_ref, wout_ref, w_sem, tsend, hot, entry_owner, entry_pos, req_ref, limit_ref, meta_ref,
     tok, pkq, pkkv, queries, fresh_all, keys, values, outgoing, csend, crecv, rsend, rrecv,
     tok_s, tok_r, q1_s, q1_r, q2_s, q2_r, k1_s, k1_r, k2_s, k2_r,
     page_s, page_r, c_s, c_r, r_s, r_r,
@@ -153,6 +184,15 @@
     n_seq, n_tp = 64, 8
     slots, page = pool_ref.shape[1], pool_ref.shape[2]
 
+    weights_in = [
+        pltpu.make_async_copy(source, into, w_sem.at[i])
+        for i, (source, into) in enumerate(
+            ((wq_hbm, wq_ref), (wkv_hbm, wkv_ref), (wout_hbm, wout_ref))
+        )
+    ]
+    for copy in weights_in:
+        copy.start()
+
     barrier = pltpu.get_barrier_semaphore()
     for k in range(1, n_tp):
         pl.semaphore_signal(
@@ -204,6 +244,8 @@
     for k in range(1, n_tp):
         token_copy(k).wait()
 
+    weights_in[0].wait()
+    weights_in[1].wait()
     square = jnp.zeros((PADDED, 1), jnp.float32)
     for i in range(n_tp):
         x = tok[i].astype(jnp.float32)
@@ -337,17 +379,20 @@
         def _():
             remote(csend.at[d], crecv.at[d], c_s.at[d], c_r.at[d], seq=d).wait()
 
-    stats = crecv[:, :, 2 * HD : 3 * HD].astype(jnp.float32)
-    came_ref[...] = stats
+    stats = crecv[:, :, 2 * HD : 3 * HD].astype(jnp.float32).reshape(n_seq * PADDED, HD)
+    third = iota((HD, 4 * HD), 0)
+    group = lax.shift_right_logical(iota((HD, 4 * HD), 1), 7)
+    gather = ones_where((third >= 3 * group) & (third < 3 * group + 3)).astype(jnp.bfloat16)
+    spread = jnp.dot(stats.astype(jnp.bfloat16), gather, preferred_element_type=jnp.float32)
+
+    def facts(j):
+        return spread[:, j * HD : (j + 1) * HD].reshape(n_seq, PADDED, HD)
+
     mixed = []
     for g in range(2):
-        def piece(j):
-            return stats[:, :, j : j + 1] + stats[:, :, j + 1 : j + 2] + stats[:, :, j + 2 : j + 3]
-
-        top = piece(6 * g)
-        peak = jnp.max(top, axis=0, keepdims=True)
-        rescale = jnp.exp(top - peak)
-        total = jnp.sum(piece(6 * g + 3) * rescale, axis=0)
+        top = facts(2 * g)
+        rescale = jnp.exp(top - jnp.max(top, axis=0, keepdims=True))
+        total = jnp.sum(facts(2 * g + 1) * rescale, axis=0)
         part = crecv[:, :, g * HD : (g + 1) * HD].astype(jnp.float32)
         summed = jnp.sum(part * rescale, axis=0)
         total = jnp.where(total > 0.0, total, 1.0)
@@ -358,6 +403,7 @@
         to = lax.rem(tp + k, n_tp)
         return remote(rsend.at[to], rrecv.at[tp], r_s.at[k], r_r.at[k], tp=to)
 
+    weights_in[2].wait()
     for i in range(n_tp):
         rsend[i] = jnp.dot(
             attended, wout_ref[:, i * width : (i + 1) * width], preferred_element_type=jnp.float32
@@ -372,41 +418,36 @@
         result = result + rrecv[i].astype(jnp.float32)
     out_ref[...] = result[0 : out_ref.shape[0], :].astype(jnp.bfloat16)
 
+    plan(stats, owner_ref, dest_ref, lengths_ref, plan_ref, n_seq, slots, page)
+
     @pl.loop(1, n_seq)
     def _(k):
         page_copy(k).wait()
 
 
-def place_kernel(from_ref, req_ref, start_ref, arrived_ref, pool_ref, fresh_ref, out_ref):
+def place_kernel(plan_ref, arrived_ref, pool_ref, fresh_ref, out_ref):
     slots, page = pool_ref.shape[1], pool_ref.shape[2]
+
+    @pl.loop(0, slots, unroll=4)
+    def _(g):
+        s = plan_ref[0, g]
+        at = jnp.maximum(s, 0)
+        where_from = jnp.full((page, HD), s, jnp.int32)
+        for c in range(2):
+            kept = jnp.where(where_from == -1, pool_ref[c, g].astype(jnp.float32), 0.0)
+            came = arrived_ref[at, c].astype(jnp.float32)
+            out_ref[c, g] = jnp.where(where_from >= 0, came, kept).astype(out_ref.dtype)
 
     @pl.loop(0, slots)
     def _(g):
-        s = from_ref[g]
-
-        @pl.when(s >= 0)
-        def _():
-            out_ref[0, g] = arrived_ref[s, 0]
-            out_ref[1, g] = arrived_ref[s, 1]
-
-        @pl.when(s == -1)
-        def _():
-            out_ref[0, g] = pool_ref[0, g]
-            out_ref[1, g] = pool_ref[1, g]
-
-        @pl.when(s < -1)
-        def _():
-            out_ref[0, g] = jnp.zeros((page, HD), out_ref.dtype)
-            out_ref[1, g] = jnp.zeros((page, HD), out_ref.dtype)
-
-        start = start_ref[g]
+        start = plan_ref[2, g]
 
         @pl.when((start > -STEPS) & (start < page))
         def _():
             ids = lax.broadcasted_iota(jnp.int32, (page, HD), 0)
             both = [out_ref[c, g].astype(jnp.float32) for c in range(2)]
             for t in range(STEPS):
-                row = req_ref[g] * STEPS + t
+                row = plan_ref[1, g] * STEPS + t
                 block = fresh_ref[lax.div(row, 6)]
                 line = lax.broadcasted_iota(jnp.int32, block.shape, 0) == lax.rem(row, 6)
                 entry = jnp.sum(jnp.where(line, block, 0.0), axis=0, keepdims=True)
@@ -443,10 +484,6 @@
         return jnp.sum(jnp.where(hot, values[None, :], 0), axis=1)
 
     pick_slot = picked(slot_ids)
-    owner_req = slot_owner[:, 0]
-    owner_page = slot_owner[:, 1]
-    base_len = take(lengths, owner_req)
-
     own_index = my_index * own_rows + jnp.arange(PADDED, dtype=i32)
     own_positions = take(lengths, own_index // STEPS) + own_index % STEPS
     frequency = ROPE_BASE ** (-jnp.arange(HD // 2, dtype=f32) * 2.0 / HD)
@@ -458,17 +495,22 @@
     rows = seq_count * PADDED
     page_shape = (seq_count, capacity, 2, page_size, HD)
     dma = pltpu.SemaphoreType.DMA
-    attn_out, arrived, came, fresh = pl.pallas_call(
+    attn_out, arrived, plan_table, fresh = pl.pallas_call(
         block_kernel,
         out_shape=[
             jax.ShapeDtypeStruct((own_rows, width), bf16),
             jax.ShapeDtypeStruct(page_shape, bf16),
-            jax.ShapeDtypeStruct((seq_count, PADDED, HD), f32),
+            jax.ShapeDtypeStruct((8, slot_count), i32),
             jax.ShapeDtypeStruct((seq_count, PADDED, 2 * HD), f32),
         ],
-        in_specs=[in_smem()] + [in_vmem()] * 11,
+        in_specs=[in_smem()] + [in_vmem()] * 2 + [pl.BlockSpec(memory_space=pl.ANY)] * 3
+        + [in_vmem()] * 6,
         out_specs=[in_vmem()] * 4,
         scratch_shapes=[
+            VMEM(w_query.shape, bf16),
+            VMEM(w_key_value.shape, bf16),
+            VMEM(w_out.shape, bf16),
+            dma((3,)),
             VMEM((PADDED, width), bf16),
             VMEM((entries, rows), bf16),
             VMEM((1, entries), f32),
@@ -509,35 +551,14 @@
         lengths[None, :],
     )
 
-    came = came[:, :capacity, 12:16].astype(i32).reshape(seq_count * capacity, 4)
-    lands = came[None, :, 0] - 1 == slot_ids[:, None]
-    landed = jnp.any(lands, axis=1)
-
-    def landing(values):
-        return jnp.sum(jnp.where(lands, values[None, :], 0), axis=1)
-
-    from_index = jnp.where(
-        landed,
-        landing(jnp.arange(seq_count * capacity, dtype=i32)),
-        jnp.where(moving, -2, -1),
-    )
-    came_req = came[:, 1]
-    came_start = take(lengths, came_req) - (came[:, 2] * 128 + came[:, 3]) * page_size
-    own_start = jnp.where(
-        (owner_req < 0) | moving, page_size, base_len - owner_page * page_size
-    )
-    final_req = jnp.where(landed, landing(came_req), owner_req)
-    final_start = jnp.where(landed, landing(came_start), own_start)
     kv_moved = pl.pallas_call(
         place_kernel,
         out_shape=jax.ShapeDtypeStruct(kv_pool.shape, kv_pool.dtype),
-        in_specs=[in_smem()] * 3 + [in_vmem()] * 3,
+        in_specs=[in_smem()] + [in_vmem()] * 3,
         out_specs=in_vmem(),
         name="place_pages",
     )(
-        from_index,
-        final_req,
-        final_start,
+        plan_table,
         arrived.reshape(seq_count * capacity, 2, page_size, HD),
         kv_pool,
         fresh,

time: 90.8 us -> 85.5 us (0.942)
  other arithmetic: 4.19 us -> 1.85 us
  local copies, waits for them, and re-layouts: 4.1 us -> 1.89 us
    unnamed x19 -> x7, local copies, waits for them, and re-layouts: 4.1 us -> 1.89 us
    pallas_call x1, Pallas kernels: 6.16 us -> 4.9 us  [local(): pl.pallas_call(place_kernel, out_shape=jax.ShapeDtypeStruct(kv_pool.shape...]
    convert_element_type x1 -> x0, other arithmetic: 1.08 us -> none  [local(): came[:, :capacity, 12:16].astype(i32).reshape(seq_count * capacity, 4)]
where the time goes in v4:
time: 85.5 us; the launch traced here: 85.3 us
  Pallas kernels  80.9 us (95%)
  local copies, waits for them, and re-layouts  1.89 us (2%)
  other arithmetic  1.85 us (2%)
    pallas_call x1, Pallas kernels, local(): pl.pallas_call(block_kernel, out_shape=[jax.ShapeDtypeStruct((own_rows, w...  76 us
    pallas_call x1, Pallas kernels, local(): pl.pallas_call(place_kernel, out_shape=jax.ShapeDtypeStruct(kv_pool.shape...  4.9 us
    unnamed x7, local copies, waits for them, and re-layouts  1.89 us

profile of v4, /device:TPU:1, one launch (start us, length us, event | category | flops | bytes accessed | tf_op | source)
XLA Modules:
  0.0 85.3 jit_solution(14963187832260438796)
XLA Ops:
  0.6 0.0 copy-start.1
  0.6 0.6 copy-done.1
  1.3 0.2 convert_reduce_fusion
  1.5 0.6 select_reduce_fusion.pick_ref
  2.1 0.0 copy-start.2
  2.2 0.6 copy-done.2
  2.8 0.2 select_reduce_fusion.1
  3.0 0.1 fusion.1
  3.1 0.7 pad_maximum_fusion
  3.8 76.0 %block.1 = (bf16[6,256]{1,0:T(8,128)(2,1)}, bf16[64,2,2,16,128]{4,3,2,1,0:T(8,128)(2,1)}, s32[8,112]{1,0:T(8,128)}, f32[64,8,256]{2,1,0:T(8,128)}) custom-call(s32[128]{0:T(128)} %select_reduce_fusion.pick_ref, bf16[6,256]{1,0:T(8,128)(2,1)} %tokens_ref.1, f32[1,2048]{1,0:T(1,128)} %bitcast.6, bf16[2048,256]{1,0:T(8,128)(2,1)} %wq_hbm.1, ...), custom_call_target="tpu_custom_call" | custom-call | tf_op jit(solution)/shard_map/block/pallas_call | solution.py:498
  79.8 0.0 copy-start
  79.8 4.9 %place_pages.1 = bf16[2,112,16,128]{3,2,1,0:T(8,128)(2,1)} custom-call(s32[8,112]{1,0:T(8,128)} %get-tuple-element.7.plan_ref, bf16[128,2,16,128]{3,2,1,0:T(8,128)(2,1)} %bitcast.5, bf16[2,112,16,128]{3,2,1,0:T(8,128)(2,1)} %pool_ref.3, f32[64,8,256]{2,1,0:T(8,128)} %get-tuple-element.9.fresh_ref), custom_call_target="tpu_custom_call" | custom-call | tf_op jit(solution)/shard_map/place_pages/pallas_call | solution.py:554
  84.7 0.0 copy-done
  84.7 0.6 copy.12
  (5 shorter events, 0.1 us)
Async XLA Ops:
  0.6 0.7 copy-start.1
  2.1 0.7 copy-start.2
  79.8 4.9 %copy-start = (bf16[6,256]{1,0:T(8,128)(2,1)S(1)}, bf16[6,256]{1,0:T(8,128)(2,1)}, u32[]{:S(2)}) copy-start(bf16[6,256]{1,0:T(8,128)(2,1)} %get-tuple-element.17) | copy-start | bytes 9220

commit v5 on v4

--- a/solution.py
+++ b/solution.py
@@ -31,7 +31,7 @@
 
 
 MESH = pl.DeviceIdType.MESH
-EARLY = 8
+EARLY = 20
 
 
 def remote(source, into, send_sem, recv_sem, **where):

time: 85.5 us -> 84.2 us (0.985)
  Pallas kernels: 80.9 us -> 79.6 us
    pallas_call x1, Pallas kernels: 76 us -> 74.7 us  [local(): pl.pallas_call(block_kernel, out_shape=[jax.ShapeDtypeStruct((own_rows, w...]
where the time goes in v5:
time: 84.2 us; the launch traced here: 84 us
  Pallas kernels  79.6 us (95%)
  local copies, waits for them, and re-layouts  1.89 us (2%)
  other arithmetic  1.85 us (2%)
    pallas_call x1, Pallas kernels, local(): pl.pallas_call(block_kernel, out_shape=[jax.ShapeDtypeStruct((own_rows, w...  74.7 us
    pallas_call x1, Pallas kernels, local(): pl.pallas_call(place_kernel, out_shape=jax.ShapeDtypeStruct(kv_pool.shape...  4.88 us
    unnamed x7, local copies, waits for them, and re-layouts  1.89 us

profile of v5, /device:TPU:1, one launch (start us, length us, event | category | flops | bytes accessed | tf_op | source)
XLA Modules:
  0.0 84.0 jit_solution(436326290121082484)
XLA Ops:
  0.6 0.0 copy-start.1
  0.6 0.6 copy-done.1
  1.3 0.2 convert_reduce_fusion
  1.5 0.6 select_reduce_fusion.pick_ref
  2.1 0.0 copy-start.2
  2.2 0.6 copy-done.2
  2.8 0.2 select_reduce_fusion.1
  3.0 0.1 fusion.1
  3.1 0.7 pad_maximum_fusion
  3.8 74.7 %block.1 = (bf16[6,256]{1,0:T(8,128)(2,1)}, bf16[64,2,2,16,128]{4,3,2,1,0:T(8,128)(2,1)}, s32[8,112]{1,0:T(8,128)}, f32[64,8,256]{2,1,0:T(8,128)}) custom-call(s32[128]{0:T(128)} %select_reduce_fusion.pick_ref, bf16[6,256]{1,0:T(8,128)(2,1)} %tokens_ref.1, f32[1,2048]{1,0:T(1,128)} %bitcast.6, bf16[2048,256]{1,0:T(8,128)(2,1)} %wq_hbm.1, ...), custom_call_target="tpu_custom_call" | custom-call | tf_op jit(solution)/shard_map/block/pallas_call | solution.py:498
  78.5 0.0 copy-start
  78.5 4.9 %place_pages.1 = bf16[2,112,16,128]{3,2,1,0:T(8,128)(2,1)} custom-call(s32[8,112]{1,0:T(8,128)} %get-tuple-element.7.plan_ref, bf16[128,2,16,128]{3,2,1,0:T(8,128)(2,1)} %bitcast.5, bf16[2,112,16,128]{3,2,1,0:T(8,128)(2,1)} %pool_ref.3, f32[64,8,256]{2,1,0:T(8,128)} %get-tuple-element.9.fresh_ref), custom_call_target="tpu_custom_call" | custom-call | tf_op jit(solution)/shard_map/place_pages/pallas_call | solution.py:554
  83.4 0.0 copy-done
  83.4 0.6 copy.12
  (5 shorter events, 0.1 us)
Async XLA Ops:
  0.6 0.7 copy-start.1
  2.1 0.7 copy-start.2
  78.5 4.9 %copy-start = (bf16[6,256]{1,0:T(8,128)(2,1)S(1)}, bf16[6,256]{1,0:T(8,128)(2,1)}, u32[]{:S(2)}) copy-start(bf16[6,256]{1,0:T(8,128)(2,1)} %get-tuple-element.17) | copy-start | bytes 9220
